TPU v7x, 512 devices: a whole 4x8x8 slice. The times are simulated.
512 devices in a mesh: grp: 4 (over x), gx: 8 (over y_hi, core), gy: 16 (over z, y_lo).
Axes of the slice: x: 4, y: 8 (y_hi: 4, y_lo: 2; y = y_hi * 2 + y_lo), z: 8, core: 2. Of those that a mesh axis runs over, the one named last changes fastest.
Arguments:
- source_term: float32 [64, 256, 1024], P('gx', 'gy', 'grp'), may hold values from -6 to 6
- conductivity: float32 [64, 256, 1024], P('gx', 'gy', 'grp'), may hold values from 0.5 to 4
- initial_field: float32 [64, 256, 1024], P('gx', 'gy', 'grp'), may hold values from -6 to 6
Outputs:
- solution: float32 [64, 256, 1024], P('gx', 'gy', 'grp')
All inputs are finite; a program needn't handle non-finite values.
Results may differ from a plain program's by a relative error of at most 0.0001.
Values sent between devices are 32-bit elements; how exact they have to be, the bound alone decides.
A program may use at most 64 MiB of HBM per device.

v0:
```python
import jax
import jax.numpy as jnp
from jax import lax
from jax.sharding import PartitionSpec as P

ITERS = 2


FIRST_RATE = 0.8
CARRY_RATE = 9.0 / 41.0
FRESH_RATE = 40.0 / 41.0


def extended(cells, sides, width):
    for axis, dim in sides:
        count = lax.axis_size(axis)
        ends = count - 1
        head = lax.slice_in_dim(cells, 0, width, axis=dim)
        tail = lax.slice_in_dim(cells, cells.shape[dim] - width, cells.shape[dim], axis=dim)
        cells = jnp.concatenate(
            [
                lax.ppermute(tail, axis, [(i, (i + 1) % count) for i in range(ends)]),
                cells,
                lax.ppermute(head, axis, [((i + 1) % count, i) for i in range(ends)]),
            ],
            axis=dim,
        )
    return cells


def neighbours(padded):
    return [
        padded[:-2, 1:-1, 1:-1],
        padded[2:, 1:-1, 1:-1],
        padded[1:-1, :-2, 1:-1],
        padded[1:-1, 2:, 1:-1],
        padded[1:-1, 1:-1, :-2],
        padded[1:-1, 1:-1, 2:],
    ]


def apply_operator(field_pad, cond_pad):
    center_field = field_pad[1:-1, 1:-1, 1:-1]
    center_cond = cond_pad[1:-1, 1:-1, 1:-1]
    result = jnp.zeros_like(center_field)
    for near_field, near_cond in zip(neighbours(field_pad), neighbours(cond_pad)):
        result = result + 0.5 * (center_cond + near_cond) * (center_field - near_field)
    return result


def diagonal_of(cond_pad):
    center_cond = cond_pad[1:-1, 1:-1, 1:-1]
    result = jnp.zeros_like(center_cond)
    for near_cond in neighbours(cond_pad):
        result = result + 0.5 * (center_cond + near_cond)
    return result


def block_mean(field):
    sizea, sizeb, sizec = field.shape
    return field.reshape(sizea // 2, 2, sizeb // 2, 2, sizec // 2, 2).mean(axis=(1, 3, 5))


def prolong(coarse):
    sizea, sizeb, sizec = coarse.shape
    spread = jnp.broadcast_to(coarse[:, None, :, None, :, None], (sizea, 2, sizeb, 2, sizec, 2))
    return spread.reshape(2 * sizea, 2 * sizeb, 2 * sizec)


def finish(residual, first, first_pad, cond_pad, diagonal):
    image = 0.25 * apply_operator(first_pad, cond_pad)
    second = CARRY_RATE * first + FRESH_RATE * (residual - image) / diagonal
    return first + second


def shards(source_term, conductivity, initial_field):
    coarse_cond = block_mean(conductivity)
    coarse_pad = extended(coarse_cond, (("grp", 2), ("gx", 0), ("gy", 1)), 1)
    coarse_diag = 0.25 * diagonal_of(coarse_pad)
    cond_pad = extended(conductivity, (("grp", 2), ("gx", 0), ("gy", 1)), 1)
    fine_diag = diagonal_of(cond_pad)
    field = initial_field
    for iteration in range(ITERS):
        field_pad = extended(field, (("grp", 2), ("gx", 0), ("gy", 1)), 1)
        residual = source_term - apply_operator(field_pad, cond_pad)
        first = FIRST_RATE * residual / fine_diag
        first_pad = extended(first, (("grp", 2), ("gx", 0), ("gy", 1)), 1)
        image = apply_operator(first_pad, cond_pad)
        fine_corr = first + (CARRY_RATE * first + FRESH_RATE * (residual - image) / fine_diag)
        coarse_res = block_mean(residual)
        coarse_first = FIRST_RATE * coarse_res / coarse_diag
        coarse_first_pad = extended(coarse_first, (("grp", 2), ("gx", 0), ("gy", 1)), 1)
        coarse_corr = finish(coarse_res, coarse_first, coarse_first_pad, coarse_pad, coarse_diag)
        field = field + fine_corr + prolong(coarse_corr)
    return field


def solution(mesh):
    return jax.shard_map(
        shards,
        mesh=mesh,
        in_specs=(P("gx", "gy", "grp"), P("gx", "gy", "grp"), P("gx", "gy", "grp")),
        out_specs=P("gx", "gy", "grp"),
        check_vma=False,
    )
```

profile of v0, /device:TPU:219, one launch (start us, length us, event | category | flops | bytes accessed | tf_op | source)
XLA Modules:
  0.0 240.7 jit_solution(211237544637983624)
XLA Ops:
  1.0 2.2 collective-permute-start.1
  3.1 3.1 %collective-permute-start = (f32[8,16,1]{2,1,0:T(8,128)S(1)}, f32[8,16,1]{2,1,0:T(8,128)S(1)}, u32[]{:S(2)}, u32[]{:S(2)}) collective-permute-start(f32[8,16,1]{2,1,0:T(8,128)S(1)} %get-tuple-element.42), channel_id=1, source_target_pairs={{0,128},{128,256},{256,384},{1,129},{129,257},{257,385},{2,130},{1... | collective-permute-start | bytes 1544 | tf_op jit(solution)/shard_map/ppermute | solution.py:22
  7.2 2.3 collective-permute-start.4
  9.5 10.5 %reshape.18 = f32[4,2,8,2,128,2]{5,4,3,2,1,0:T(8,128)} reshape(f32[8,16,256]{2,1,0:T(8,128)} %param.4) | data formatting | bytes 262144 | tf_op jit(solution)/shard_map/reshape | solution.py:61
  20.1 4.0 %reduce_sum.28 = f32[4,8,128]{2,1,0:T(8,128)S(1)} reduce(f32[4,2,8,2,128,2]{5,4,3,2,1,0:T(8,128)} %reshape.18, f32[]{:T(128)} %constant.6.clone.1), dimensions={1,3,5}, to_apply=%region_1.0 | reduce | flops 28672 | bytes 147460 | tf_op jit(solution)/shard_map/reduce_sum | solution.py:61
  26.1 3.4 %collective-permute-start.18 = (f32[4,8,1]{2,1,0:T(8,128)S(1)}, f32[4,8,1]{2,1,0:T(8,128)S(1)}, u32[]{:S(2)}, u32[]{:S(2)}) collective-permute-start(f32[4,8,1]{2,1,0:T(8,128)S(1)} %get-tuple-element.60), channel_id=1, source_target_pairs={{0,128},{128,256},{256,384},{1,129},{129,257},{257,385},{2,130},{1... | collective-permute-start | bytes 392 | tf_op jit(solution)/shard_map/ppermute | solution.py:22
  29.5 3.1 %collective-permute-start.3 = (f32[8,16,1]{2,1,0:T(8,128)S(1)}, f32[8,16,1]{2,1,0:T(8,128)S(1)}, u32[]{:S(2)}, u32[]{:S(2)}) collective-permute-start(f32[8,16,1]{2,1,0:T(8,128)S(1)} %get-tuple-element.40), channel_id=1, source_target_pairs={{0,128},{128,256},{256,384},{1,129},{129,257},{257,385},{2,130},{1... | collective-permute-start | bytes 1544 | tf_op jit(solution)/shard_map/ppermute | solution.py:22
  32.7 6.8 %collective-permute-start.20 = (f32[1,8,130]{2,1,0:T(8,128)S(1)}, f32[1,8,130]{2,1,0:T(8,128)S(1)}, u32[]{:S(2)}, u32[]{:S(2)}) collective-permute-start(f32[1,8,130]{2,1,0:T(8,128)S(1)} %get-tuple-element.55), channel_id=1, source_target_pairs={{0,16},{16,32},{32,48},{48,64},{64,80},{80,96},{96,112},{1,17},{17... | collective-permute-start | bytes 12488 | tf_op jit(solution)/shard_map/ppermute | solution.py:22
  39.4 1.9 collective-permute-start.21
  41.5 2.0 collective-permute-start.7
  43.5 5.6 %collective-permute-start.5 = (f32[1,16,258]{2,1,0:T(8,128)S(1)}, f32[1,16,258]{2,1,0:T(8,128)S(1)}, u32[]{:S(2)}, u32[]{:S(2)}) collective-permute-start(f32[1,16,258]{2,1,0:T(8,128)S(1)} %get-tuple-element.32), channel_id=1, source_target_pairs={{0,16},{16,32},{32,48},{48,64},{64,80},{80,96},{96,112},{1,17},{17... | collective-permute-start | bytes 49544 | tf_op jit(solution)/shard_map/ppermute | solution.py:22
  49.3 2.4 collective-permute-start.2
  51.7 1.9 collective-permute-start.6
  53.8 3.0 %collective-permute-start.11 = (f32[10,1,258]{2,1,0:T(1,128)S(1)}, f32[10,1,258]{2,1,0:T(1,128)S(1)}, u32[]{:S(2)}, u32[]{:S(2)}) collective-permute-start(f32[10,1,258]{2,1,0:T(1,128)S(1)} %get-tuple-element.23), channel_id=1, source_target_pairs={{1,0},{2,1},{3,2},{4,3},{5,4},{6,5},{7,6},{8,7},{9,8},{10,9},{11,1... | collective-permute-start | bytes 30968 | tf_op jit(solution)/shard_map/ppermute | solution.py:24
  56.8 4.9 %collective-permute-start.9 = (f32[10,1,258]{2,1,0:T(1,128)S(1)}, f32[10,1,258]{2,1,0:T(1,128)S(1)}, u32[]{:S(2)}, u32[]{:S(2)}) collective-permute-start(f32[10,1,258]{2,1,0:T(1,128)S(1)} %get-tuple-element.22), channel_id=1, source_target_pairs={{0,1},{1,2},{2,3},{3,4},{4,5},{5,6},{6,7},{7,8},{8,9},{9,10},{10,1... | collective-permute-start | bytes 30968 | tf_op jit(solution)/shard_map/ppermute | solution.py:22
  61.9 3.5 %collective-permute-start.8 = (f32[10,1,258]{2,1,0:T(1,128)S(1)}, f32[10,1,258]{2,1,0:T(1,128)S(1)}, u32[]{:S(2)}, u32[]{:S(2)}) collective-permute-start(f32[10,1,258]{2,1,0:T(1,128)S(1)} %get-tuple-element.21), channel_id=1, source_target_pairs={{0,1},{1,2},{2,3},{3,4},{4,5},{5,6},{6,7},{7,8},{8,9},{9,10},{10,1... | collective-permute-start | bytes 30968 | tf_op jit(solution)/shard_map/ppermute | solution.py:22
  67.4 5.5 %collective-permute-start.22 = (f32[6,1,130]{2,1,0:T(1,128)S(1)}, f32[6,1,130]{2,1,0:T(1,128)S(1)}, u32[]{:S(2)}, u32[]{:S(2)}) collective-permute-start(f32[6,1,130]{2,1,0:T(1,128)S(1)} %get-tuple-element.49), channel_id=1, source_target_pairs={{0,1},{1,2},{2,3},{3,4},{4,5},{5,6},{6,7},{7,8},{8,9},{9,10},{10,1... | collective-permute-start | bytes 9368 | tf_op jit(solution)/shard_map/ppermute | solution.py:22
  72.9 1.9 collective-permute-start.23
  75.4 9.8 %reshape.17 = f32[4,2,8,2,128,2]{5,4,3,2,1,0:T(8,128)} reshape(f32[8,16,256]{2,1,0:T(8,128)S(1)} %get-tuple-element.9) | data formatting | bytes 262144 | tf_op jit(solution)/shard_map/reshape | solution.py:61
  85.1 4.0 %reduce_sum.27 = f32[4,8,128]{2,1,0:T(8,128)S(1)} reduce(f32[4,2,8,2,128,2]{5,4,3,2,1,0:T(8,128)} %reshape.17, f32[]{:T(128)} %constant.6.clone.1), dimensions={1,3,5}, to_apply=%region_0.0 | reduce | flops 28672 | bytes 147460 | tf_op jit(solution)/shard_map/reduce_sum | solution.py:61
  89.4 2.2 collective-permute-start.25
  91.5 3.1 %collective-permute-start.24 = (f32[4,8,1]{2,1,0:T(8,128)S(1)}, f32[4,8,1]{2,1,0:T(8,128)S(1)}, u32[]{:S(2)}, u32[]{:S(2)}) collective-permute-start(f32[4,8,1]{2,1,0:T(8,128)S(1)} %get-tuple-element.58), channel_id=1, source_target_pairs={{0,128},{128,256},{256,384},{1,129},{129,257},{257,385},{2,130},{1... | collective-permute-start | bytes 392 | tf_op jit(solution)/shard_map/ppermute | solution.py:22
  94.7 2.2 collective-permute-start.13
  96.9 3.1 %collective-permute-start.12 = (f32[8,16,1]{2,1,0:T(8,128)S(1)}, f32[8,16,1]{2,1,0:T(8,128)S(1)}, u32[]{:S(2)}, u32[]{:S(2)}) collective-permute-start(f32[8,16,1]{2,1,0:T(8,128)S(1)} %get-tuple-element.38), channel_id=1, source_target_pairs={{0,128},{128,256},{256,384},{1,129},{129,257},{257,385},{2,130},{1... | collective-permute-start | bytes 1544 | tf_op jit(solution)/shard_map/ppermute | solution.py:22
  100.1 4.3 %collective-permute-start.27 = (f32[1,8,130]{2,1,0:T(8,128)S(1)}, f32[1,8,130]{2,1,0:T(8,128)S(1)}, u32[]{:S(2)}, u32[]{:S(2)}) collective-permute-start(f32[1,8,130]{2,1,0:T(8,128)S(1)} %get-tuple-element.53), channel_id=1, source_target_pairs={{16,0},{32,16},{48,32},{64,48},{80,64},{96,80},{112,96},{17,1},{33... | collective-permute-start | bytes 12488 | tf_op jit(solution)/shard_map/ppermute | solution.py:24
  104.5 5.8 %collective-permute-start.26 = (f32[1,8,130]{2,1,0:T(8,128)S(1)}, f32[1,8,130]{2,1,0:T(8,128)S(1)}, u32[]{:S(2)}, u32[]{:S(2)}) collective-permute-start(f32[1,8,130]{2,1,0:T(8,128)S(1)} %get-tuple-element.52), channel_id=1, source_target_pairs={{0,16},{16,32},{32,48},{48,64},{64,80},{80,96},{96,112},{1,17},{17... | collective-permute-start | bytes 12488 | tf_op jit(solution)/shard_map/ppermute | solution.py:22
  110.3 1.9 collective-permute-start.15
  112.3 5.8 %collective-permute-start.14 = (f32[1,16,258]{2,1,0:T(8,128)S(1)}, f32[1,16,258]{2,1,0:T(8,128)S(1)}, u32[]{:S(2)}, u32[]{:S(2)}) collective-permute-start(f32[1,16,258]{2,1,0:T(8,128)S(1)} %get-tuple-element.28), channel_id=1, source_target_pairs={{0,16},{16,32},{32,48},{48,64},{64,80},{80,96},{96,112},{1,17},{17... | collective-permute-start | bytes 49544 | tf_op jit(solution)/shard_map/ppermute | solution.py:22
  120.1 5.8 %collective-permute-start.28 = (f32[6,1,130]{2,1,0:T(1,128)S(1)}, f32[6,1,130]{2,1,0:T(1,128)S(1)}, u32[]{:S(2)}, u32[]{:S(2)}) collective-permute-start(f32[6,1,130]{2,1,0:T(1,128)S(1)} %get-tuple-element.46), channel_id=1, source_target_pairs={{0,1},{1,2},{2,3},{3,4},{4,5},{5,6},{6,7},{7,8},{8,9},{9,10},{10,1... | collective-permute-start | bytes 9368 | tf_op jit(solution)/shard_map/ppermute | solution.py:22
  127.9 5.5 %collective-permute-start.16 = (f32[10,1,258]{2,1,0:T(1,128)S(1)}, f32[10,1,258]{2,1,0:T(1,128)S(1)}, u32[]{:S(2)}, u32[]{:S(2)}) collective-permute-start(f32[10,1,258]{2,1,0:T(1,128)S(1)} %get-tuple-element.18), channel_id=1, source_target_pairs={{0,1},{1,2},{2,3},{3,4},{4,5},{5,6},{6,7},{7,8},{8,9},{9,10},{10,1... | collective-permute-start | bytes 30968 | tf_op jit(solution)/shard_map/ppermute | solution.py:22
  133.6 3.9 %broadcast_in_dim.4 = f32[4,2,8,2,128,2]{5,4,3,2,1,0:T(8,128)} broadcast(f32[4,8,128]{2,1,0:T(8,128)S(1)} %fusion.127), dimensions={0,2,4} | broadcast | bytes 147456 | tf_op jit(solution)/shard_map/broadcast_in_dim | solution.py:66
  137.5 6.9 %reshape.19 = f32[8,16,256]{2,1,0:T(8,128)S(1)} reshape(f32[4,2,8,2,128,2]{5,4,3,2,1,0:T(8,128)} %broadcast_in_dim.4) | data formatting | bytes 262144 | tf_op jit(solution)/shard_map/reshape | solution.py:67
  144.9 2.2 collective-permute-start.31
  147.0 3.1 %collective-permute-start.30 = (f32[8,16,1]{2,1,0:T(8,128)S(1)}, f32[8,16,1]{2,1,0:T(8,128)S(1)}, u32[]{:S(2)}, u32[]{:S(2)}) collective-permute-start(f32[8,16,1]{2,1,0:T(8,128)S(1)} %get-tuple-element.36), channel_id=1, source_target_pairs={{0,128},{128,256},{256,384},{1,129},{129,257},{257,385},{2,130},{1... | collective-permute-start | bytes 1544 | tf_op jit(solution)/shard_map/ppermute | solution.py:22
  154.1 5.8 %collective-permute-start.32 = (f32[1,16,258]{2,1,0:T(8,128)S(1)}, f32[1,16,258]{2,1,0:T(8,128)S(1)}, u32[]{:S(2)}, u32[]{:S(2)}) collective-permute-start(f32[1,16,258]{2,1,0:T(8,128)S(1)} %get-tuple-element.26), channel_id=1, source_target_pairs={{0,16},{16,32},{32,48},{48,64},{64,80},{80,96},{96,112},{1,17},{17... | collective-permute-start | bytes 49544 | tf_op jit(solution)/shard_map/ppermute | solution.py:22
  162.8 5.5 %collective-permute-start.34 = (f32[10,1,258]{2,1,0:T(1,128)S(1)}, f32[10,1,258]{2,1,0:T(1,128)S(1)}, u32[]{:S(2)}, u32[]{:S(2)}) collective-permute-start(f32[10,1,258]{2,1,0:T(1,128)S(1)} %get-tuple-element.16), channel_id=1, source_target_pairs={{0,1},{1,2},{2,3},{3,4},{4,5},{5,6},{6,7},{7,8},{8,9},{9,10},{10,1... | collective-permute-start | bytes 30968 | tf_op jit(solution)/shard_map/ppermute | solution.py:22
  169.5 9.8 %reshape.20 = f32[4,2,8,2,128,2]{5,4,3,2,1,0:T(8,128)} reshape(f32[8,16,256]{2,1,0:T(8,128)S(1)} %get-tuple-element.6) | data formatting | bytes 262144 | tf_op jit(solution)/shard_map/reshape | solution.py:61
  179.3 4.0 %reduce_sum.29 = f32[4,8,128]{2,1,0:T(8,128)S(1)} reduce(f32[4,2,8,2,128,2]{5,4,3,2,1,0:T(8,128)} %reshape.20, f32[]{:T(128)} %constant.6.clone.1), dimensions={1,3,5}, to_apply=%region_2.0 | reduce | flops 28672 | bytes 147460 | tf_op jit(solution)/shard_map/reduce_sum | solution.py:61
  185.4 3.5 %collective-permute-start.42 = (f32[4,8,1]{2,1,0:T(8,128)S(1)}, f32[4,8,1]{2,1,0:T(8,128)S(1)}, u32[]{:S(2)}, u32[]{:S(2)}) collective-permute-start(f32[4,8,1]{2,1,0:T(8,128)S(1)} %get-tuple-element.56), channel_id=1, source_target_pairs={{0,128},{128,256},{256,384},{1,129},{129,257},{257,385},{2,130},{1... | collective-permute-start | bytes 392 | tf_op jit(solution)/shard_map/ppermute | solution.py:22
  191.0 3.4 %collective-permute-start.36 = (f32[8,16,1]{2,1,0:T(8,128)S(1)}, f32[8,16,1]{2,1,0:T(8,128)S(1)}, u32[]{:S(2)}, u32[]{:S(2)}) collective-permute-start(f32[8,16,1]{2,1,0:T(8,128)S(1)} %get-tuple-element.34), channel_id=1, source_target_pairs={{0,128},{128,256},{256,384},{1,129},{129,257},{257,385},{2,130},{1... | collective-permute-start | bytes 1544 | tf_op jit(solution)/shard_map/ppermute | solution.py:22
  194.4 2.5 %collective-permute-start.45 = (f32[1,8,130]{2,1,0:T(8,128)S(1)}, f32[1,8,130]{2,1,0:T(8,128)S(1)}, u32[]{:S(2)}, u32[]{:S(2)}) collective-permute-start(f32[1,8,130]{2,1,0:T(8,128)S(1)} %get-tuple-element.51), channel_id=1, source_target_pairs={{16,0},{32,16},{48,32},{64,48},{80,64},{96,80},{112,96},{17,1},{33... | collective-permute-start | bytes 12488 | tf_op jit(solution)/shard_map/ppermute | solution.py:24
  196.9 8.0 %collective-permute-start.44 = (f32[1,8,130]{2,1,0:T(8,128)S(1)}, f32[1,8,130]{2,1,0:T(8,128)S(1)}, u32[]{:S(2)}, u32[]{:S(2)}) collective-permute-start(f32[1,8,130]{2,1,0:T(8,128)S(1)} %get-tuple-element.50), channel_id=1, source_target_pairs={{0,16},{16,32},{32,48},{48,64},{64,80},{80,96},{96,112},{1,17},{17... | collective-permute-start | bytes 12488 | tf_op jit(solution)/shard_map/ppermute | solution.py:22
  207.0 5.8 %collective-permute-start.38 = (f32[1,16,258]{2,1,0:T(8,128)S(1)}, f32[1,16,258]{2,1,0:T(8,128)S(1)}, u32[]{:S(2)}, u32[]{:S(2)}) collective-permute-start(f32[1,16,258]{2,1,0:T(8,128)S(1)} %get-tuple-element.24), channel_id=1, source_target_pairs={{0,16},{16,32},{32,48},{48,64},{64,80},{80,96},{96,112},{1,17},{17... | collective-permute-start | bytes 49544 | tf_op jit(solution)/shard_map/ppermute | solution.py:22
  214.8 6.0 %collective-permute-start.46 = (f32[6,1,130]{2,1,0:T(1,128)S(1)}, f32[6,1,130]{2,1,0:T(1,128)S(1)}, u32[]{:S(2)}, u32[]{:S(2)}) collective-permute-start(f32[6,1,130]{2,1,0:T(1,128)S(1)} %get-tuple-element.44), channel_id=1, source_target_pairs={{0,1},{1,2},{2,3},{3,4},{4,5},{5,6},{6,7},{7,8},{8,9},{9,10},{10,1... | collective-permute-start | bytes 9368 | tf_op jit(solution)/shard_map/ppermute | solution.py:22
  221.0 1.9 collective-permute-start.41
  222.9 5.5 %collective-permute-start.40 = (f32[10,1,258]{2,1,0:T(1,128)S(1)}, f32[10,1,258]{2,1,0:T(1,128)S(1)}, u32[]{:S(2)}, u32[]{:S(2)}) collective-permute-start(f32[10,1,258]{2,1,0:T(1,128)S(1)} %get-tuple-element.14), channel_id=1, source_target_pairs={{0,1},{1,2},{2,3},{3,4},{4,5},{5,6},{6,7},{7,8},{8,9},{9,10},{10,1... | collective-permute-start | bytes 30968 | tf_op jit(solution)/shard_map/ppermute | solution.py:22
  228.6 3.9 %broadcast_in_dim.5 = f32[4,2,8,2,128,2]{5,4,3,2,1,0:T(8,128)} broadcast(f32[4,8,128]{2,1,0:T(8,128)S(1)} %fusion.104), dimensions={0,2,4} | broadcast | bytes 147456 | tf_op jit(solution)/shard_map/broadcast_in_dim | solution.py:66
  232.5 6.9 %reshape.21 = f32[8,16,256]{2,1,0:T(8,128)S(1)} reshape(f32[4,2,8,2,128,2]{5,4,3,2,1,0:T(8,128)} %broadcast_in_dim.5) | data formatting | bytes 262144 | tf_op jit(solution)/shard_map/reshape | solution.py:67
  (97 shorter events, 29.8 us)
Async XLA Ops:
  1.0 42.6 %collective-permute-start.1 = (f32[8,16,1]{2,1,0:T(8,128)S(1)}, f32[8,16,1]{2,1,0:T(8,128)S(1)}, u32[]{:S(2)}, u32[]{:S(2)}) collective-permute-start(f32[8,16,1]{2,1,0:T(8,128)S(1)} %get-tuple-element.43), channel_id=1, source_target_pairs={{128,0},{256,128},{384,256},{129,1},{257,129},{385,257},{130,2},{2... | collective-permute-start | bytes 1544 | tf_op jit(solution)/shard_map/ppermute | solution.py:24
  3.1 46.1 %collective-permute-start = (f32[8,16,1]{2,1,0:T(8,128)S(1)}, f32[8,16,1]{2,1,0:T(8,128)S(1)}, u32[]{:S(2)}, u32[]{:S(2)}) collective-permute-start(f32[8,16,1]{2,1,0:T(8,128)S(1)} %get-tuple-element.42), channel_id=1, source_target_pairs={{0,128},{128,256},{256,384},{1,129},{129,257},{257,385},{2,130},{1... | collective-permute-start | bytes 1544 | tf_op jit(solution)/shard_map/ppermute | solution.py:22
  7.2 32.2 %collective-permute-start.4 = (f32[8,16,1]{2,1,0:T(8,128)S(1)}, f32[8,16,1]{2,1,0:T(8,128)S(1)}, u32[]{:S(2)}, u32[]{:S(2)}) collective-permute-start(f32[8,16,1]{2,1,0:T(8,128)S(1)} %get-tuple-element.41), channel_id=1, source_target_pairs={{128,0},{256,128},{384,256},{129,1},{257,129},{385,257},{130,2},{2... | collective-permute-start | bytes 1544 | tf_op jit(solution)/shard_map/ppermute | solution.py:24
  24.2 5.3 %collective-permute-start.19 = (f32[4,8,1]{2,1,0:T(8,128)S(1)}, f32[4,8,1]{2,1,0:T(8,128)S(1)}, u32[]{:S(2)}, u32[]{:S(2)}) collective-permute-start(f32[4,8,1]{2,1,0:T(8,128)S(1)} %get-tuple-element.61), channel_id=1, source_target_pairs={{128,0},{256,128},{384,256},{129,1},{257,129},{385,257},{130,2},{2... | collective-permute-start | bytes 392 | tf_op jit(solution)/shard_map/ppermute | solution.py:24
  26.1 6.5 %collective-permute-start.18 = (f32[4,8,1]{2,1,0:T(8,128)S(1)}, f32[4,8,1]{2,1,0:T(8,128)S(1)}, u32[]{:S(2)}, u32[]{:S(2)}) collective-permute-start(f32[4,8,1]{2,1,0:T(8,128)S(1)} %get-tuple-element.60), channel_id=1, source_target_pairs={{0,128},{128,256},{256,384},{1,129},{129,257},{257,385},{2,130},{1... | collective-permute-start | bytes 392 | tf_op jit(solution)/shard_map/ppermute | solution.py:22
  29.5 11.9 %collective-permute-start.3 = (f32[8,16,1]{2,1,0:T(8,128)S(1)}, f32[8,16,1]{2,1,0:T(8,128)S(1)}, u32[]{:S(2)}, u32[]{:S(2)}) collective-permute-start(f32[8,16,1]{2,1,0:T(8,128)S(1)} %get-tuple-element.40), channel_id=1, source_target_pairs={{0,128},{128,256},{256,384},{1,129},{129,257},{257,385},{2,130},{1... | collective-permute-start | bytes 1544 | tf_op jit(solution)/shard_map/ppermute | solution.py:22
  32.7 32.7 %collective-permute-start.20 = (f32[1,8,130]{2,1,0:T(8,128)S(1)}, f32[1,8,130]{2,1,0:T(8,128)S(1)}, u32[]{:S(2)}, u32[]{:S(2)}) collective-permute-start(f32[1,8,130]{2,1,0:T(8,128)S(1)} %get-tuple-element.55), channel_id=1, source_target_pairs={{0,16},{16,32},{32,48},{48,64},{64,80},{80,96},{96,112},{1,17},{17... | collective-permute-start | bytes 12488 | tf_op jit(solution)/shard_map/ppermute | solution.py:22
  39.4 27.9 %collective-permute-start.21 = (f32[1,8,130]{2,1,0:T(8,128)S(1)}, f32[1,8,130]{2,1,0:T(8,128)S(1)}, u32[]{:S(2)}, u32[]{:S(2)}) collective-permute-start(f32[1,8,130]{2,1,0:T(8,128)S(1)} %get-tuple-element.54), channel_id=1, source_target_pairs={{16,0},{32,16},{48,32},{64,48},{80,64},{96,80},{112,96},{17,1},{33... | collective-permute-start | bytes 12488 | tf_op jit(solution)/shard_map/ppermute | solution.py:24
  41.5 10.2 %collective-permute-start.7 = (f32[1,16,258]{2,1,0:T(8,128)S(1)}, f32[1,16,258]{2,1,0:T(8,128)S(1)}, u32[]{:S(2)}, u32[]{:S(2)}) collective-permute-start(f32[1,16,258]{2,1,0:T(8,128)S(1)} %get-tuple-element.33), channel_id=1, source_target_pairs={{16,0},{32,16},{48,32},{64,48},{80,64},{96,80},{112,96},{17,1},{33... | collective-permute-start | bytes 49544 | tf_op jit(solution)/shard_map/ppermute | solution.py:24
  43.5 10.1 %collective-permute-start.5 = (f32[1,16,258]{2,1,0:T(8,128)S(1)}, f32[1,16,258]{2,1,0:T(8,128)S(1)}, u32[]{:S(2)}, u32[]{:S(2)}) collective-permute-start(f32[1,16,258]{2,1,0:T(8,128)S(1)} %get-tuple-element.32), channel_id=1, source_target_pairs={{0,16},{16,32},{32,48},{48,64},{64,80},{80,96},{96,112},{1,17},{17... | collective-permute-start | bytes 49544 | tf_op jit(solution)/shard_map/ppermute | solution.py:22
  49.3 7.5 %collective-permute-start.2 = (f32[1,16,258]{2,1,0:T(8,128)S(1)}, f32[1,16,258]{2,1,0:T(8,128)S(1)}, u32[]{:S(2)}, u32[]{:S(2)}) collective-permute-start(f32[1,16,258]{2,1,0:T(8,128)S(1)} %get-tuple-element.31), channel_id=1, source_target_pairs={{0,16},{16,32},{32,48},{48,64},{64,80},{80,96},{96,112},{1,17},{17... | collective-permute-start | bytes 49544 | tf_op jit(solution)/shard_map/ppermute | solution.py:22
  51.7 10.0 %collective-permute-start.6 = (f32[1,16,258]{2,1,0:T(8,128)S(1)}, f32[1,16,258]{2,1,0:T(8,128)S(1)}, u32[]{:S(2)}, u32[]{:S(2)}) collective-permute-start(f32[1,16,258]{2,1,0:T(8,128)S(1)} %get-tuple-element.30), channel_id=1, source_target_pairs={{16,0},{32,16},{48,32},{64,48},{80,64},{96,80},{112,96},{17,1},{33... | collective-permute-start | bytes 49544 | tf_op jit(solution)/shard_map/ppermute | solution.py:24
  53.8 19.1 %collective-permute-start.11 = (f32[10,1,258]{2,1,0:T(1,128)S(1)}, f32[10,1,258]{2,1,0:T(1,128)S(1)}, u32[]{:S(2)}, u32[]{:S(2)}) collective-permute-start(f32[10,1,258]{2,1,0:T(1,128)S(1)} %get-tuple-element.23), channel_id=1, source_target_pairs={{1,0},{2,1},{3,2},{4,3},{5,4},{6,5},{7,6},{8,7},{9,8},{10,9},{11,1... | collective-permute-start | bytes 30968 | tf_op jit(solution)/shard_map/ppermute | solution.py:24
  56.8 18.1 %collective-permute-start.9 = (f32[10,1,258]{2,1,0:T(1,128)S(1)}, f32[10,1,258]{2,1,0:T(1,128)S(1)}, u32[]{:S(2)}, u32[]{:S(2)}) collective-permute-start(f32[10,1,258]{2,1,0:T(1,128)S(1)} %get-tuple-element.22), channel_id=1, source_target_pairs={{0,1},{1,2},{2,3},{3,4},{4,5},{5,6},{6,7},{7,8},{8,9},{9,10},{10,1... | collective-permute-start | bytes 30968 | tf_op jit(solution)/shard_map/ppermute | solution.py:22
  61.9 13.0 %collective-permute-start.8 = (f32[10,1,258]{2,1,0:T(1,128)S(1)}, f32[10,1,258]{2,1,0:T(1,128)S(1)}, u32[]{:S(2)}, u32[]{:S(2)}) collective-permute-start(f32[10,1,258]{2,1,0:T(1,128)S(1)} %get-tuple-element.21), channel_id=1, source_target_pairs={{0,1},{1,2},{2,3},{3,4},{4,5},{5,6},{6,7},{7,8},{8,9},{9,10},{10,1... | collective-permute-start | bytes 30968 | tf_op jit(solution)/shard_map/ppermute | solution.py:22
  65.4 9.5 %collective-permute-start.10 = (f32[10,1,258]{2,1,0:T(1,128)S(1)}, f32[10,1,258]{2,1,0:T(1,128)S(1)}, u32[]{:S(2)}, u32[]{:S(2)}) collective-permute-start(f32[10,1,258]{2,1,0:T(1,128)S(1)} %get-tuple-element.20), channel_id=1, source_target_pairs={{1,0},{2,1},{3,2},{4,3},{5,4},{6,5},{7,6},{8,7},{9,8},{10,9},{11,1... | collective-permute-start | bytes 30968 | tf_op jit(solution)/shard_map/ppermute | solution.py:24
  67.4 21.7 %collective-permute-start.22 = (f32[6,1,130]{2,1,0:T(1,128)S(1)}, f32[6,1,130]{2,1,0:T(1,128)S(1)}, u32[]{:S(2)}, u32[]{:S(2)}) collective-permute-start(f32[6,1,130]{2,1,0:T(1,128)S(1)} %get-tuple-element.49), channel_id=1, source_target_pairs={{0,1},{1,2},{2,3},{3,4},{4,5},{5,6},{6,7},{7,8},{8,9},{9,10},{10,1... | collective-permute-start | bytes 9368 | tf_op jit(solution)/shard_map/ppermute | solution.py:22
  72.9 16.3 %collective-permute-start.23 = (f32[6,1,130]{2,1,0:T(1,128)S(1)}, f32[6,1,130]{2,1,0:T(1,128)S(1)}, u32[]{:S(2)}, u32[]{:S(2)}) collective-permute-start(f32[6,1,130]{2,1,0:T(1,128)S(1)} %get-tuple-element.48), channel_id=1, source_target_pairs={{1,0},{2,1},{3,2},{4,3},{5,4},{6,5},{7,6},{8,7},{9,8},{10,9},{11,1... | collective-permute-start | bytes 9368 | tf_op jit(solution)/shard_map/ppermute | solution.py:24
  89.4 10.7 %collective-permute-start.25 = (f32[4,8,1]{2,1,0:T(8,128)S(1)}, f32[4,8,1]{2,1,0:T(8,128)S(1)}, u32[]{:S(2)}, u32[]{:S(2)}) collective-permute-start(f32[4,8,1]{2,1,0:T(8,128)S(1)} %get-tuple-element.59), channel_id=1, source_target_pairs={{128,0},{256,128},{384,256},{129,1},{257,129},{385,257},{130,2},{2... | collective-permute-start | bytes 392 | tf_op jit(solution)/shard_map/ppermute | solution.py:24
  91.5 8.5 %collective-permute-start.24 = (f32[4,8,1]{2,1,0:T(8,128)S(1)}, f32[4,8,1]{2,1,0:T(8,128)S(1)}, u32[]{:S(2)}, u32[]{:S(2)}) collective-permute-start(f32[4,8,1]{2,1,0:T(8,128)S(1)} %get-tuple-element.58), channel_id=1, source_target_pairs={{0,128},{128,256},{256,384},{1,129},{129,257},{257,385},{2,130},{1... | collective-permute-start | bytes 392 | tf_op jit(solution)/shard_map/ppermute | solution.py:22
  94.7 15.5 %collective-permute-start.13 = (f32[8,16,1]{2,1,0:T(8,128)S(1)}, f32[8,16,1]{2,1,0:T(8,128)S(1)}, u32[]{:S(2)}, u32[]{:S(2)}) collective-permute-start(f32[8,16,1]{2,1,0:T(8,128)S(1)} %get-tuple-element.39), channel_id=1, source_target_pairs={{128,0},{256,128},{384,256},{129,1},{257,129},{385,257},{130,2},{2... | collective-permute-start | bytes 1544 | tf_op jit(solution)/shard_map/ppermute | solution.py:24
  96.9 13.3 %collective-permute-start.12 = (f32[8,16,1]{2,1,0:T(8,128)S(1)}, f32[8,16,1]{2,1,0:T(8,128)S(1)}, u32[]{:S(2)}, u32[]{:S(2)}) collective-permute-start(f32[8,16,1]{2,1,0:T(8,128)S(1)} %get-tuple-element.38), channel_id=1, source_target_pairs={{0,128},{128,256},{256,384},{1,129},{129,257},{257,385},{2,130},{1... | collective-permute-start | bytes 1544 | tf_op jit(solution)/shard_map/ppermute | solution.py:22
  100.1 17.9 %collective-permute-start.27 = (f32[1,8,130]{2,1,0:T(8,128)S(1)}, f32[1,8,130]{2,1,0:T(8,128)S(1)}, u32[]{:S(2)}, u32[]{:S(2)}) collective-permute-start(f32[1,8,130]{2,1,0:T(8,128)S(1)} %get-tuple-element.53), channel_id=1, source_target_pairs={{16,0},{32,16},{48,32},{64,48},{80,64},{96,80},{112,96},{17,1},{33... | collective-permute-start | bytes 12488 | tf_op jit(solution)/shard_map/ppermute | solution.py:24
  104.5 13.6 %collective-permute-start.26 = (f32[1,8,130]{2,1,0:T(8,128)S(1)}, f32[1,8,130]{2,1,0:T(8,128)S(1)}, u32[]{:S(2)}, u32[]{:S(2)}) collective-permute-start(f32[1,8,130]{2,1,0:T(8,128)S(1)} %get-tuple-element.52), channel_id=1, source_target_pairs={{0,16},{16,32},{32,48},{48,64},{64,80},{80,96},{96,112},{1,17},{17... | collective-permute-start | bytes 12488 | tf_op jit(solution)/shard_map/ppermute | solution.py:22
  110.3 15.5 %collective-permute-start.15 = (f32[1,16,258]{2,1,0:T(8,128)S(1)}, f32[1,16,258]{2,1,0:T(8,128)S(1)}, u32[]{:S(2)}, u32[]{:S(2)}) collective-permute-start(f32[1,16,258]{2,1,0:T(8,128)S(1)} %get-tuple-element.29), channel_id=1, source_target_pairs={{16,0},{32,16},{48,32},{64,48},{80,64},{96,80},{112,96},{17,1},{33... | collective-permute-start | bytes 49544 | tf_op jit(solution)/shard_map/ppermute | solution.py:24
  112.3 13.6 %collective-permute-start.14 = (f32[1,16,258]{2,1,0:T(8,128)S(1)}, f32[1,16,258]{2,1,0:T(8,128)S(1)}, u32[]{:S(2)}, u32[]{:S(2)}) collective-permute-start(f32[1,16,258]{2,1,0:T(8,128)S(1)} %get-tuple-element.28), channel_id=1, source_target_pairs={{0,16},{16,32},{32,48},{48,64},{64,80},{80,96},{96,112},{1,17},{17... | collective-permute-start | bytes 49544 | tf_op jit(solution)/shard_map/ppermute | solution.py:22
  118.1 15.3 %collective-permute-start.29 = (f32[6,1,130]{2,1,0:T(1,128)S(1)}, f32[6,1,130]{2,1,0:T(1,128)S(1)}, u32[]{:S(2)}, u32[]{:S(2)}) collective-permute-start(f32[6,1,130]{2,1,0:T(1,128)S(1)} %get-tuple-element.47), channel_id=1, source_target_pairs={{1,0},{2,1},{3,2},{4,3},{5,4},{6,5},{7,6},{8,7},{9,8},{10,9},{11,1... | collective-permute-start | bytes 9368 | tf_op jit(solution)/shard_map/ppermute | solution.py:24
  120.1 13.3 %collective-permute-start.28 = (f32[6,1,130]{2,1,0:T(1,128)S(1)}, f32[6,1,130]{2,1,0:T(1,128)S(1)}, u32[]{:S(2)}, u32[]{:S(2)}) collective-permute-start(f32[6,1,130]{2,1,0:T(1,128)S(1)} %get-tuple-element.46), channel_id=1, source_target_pairs={{0,1},{1,2},{2,3},{3,4},{4,5},{5,6},{6,7},{7,8},{8,9},{9,10},{10,1... | collective-permute-start | bytes 9368 | tf_op jit(solution)/shard_map/ppermute | solution.py:22
  126.0 18.4 %collective-permute-start.17 = (f32[10,1,258]{2,1,0:T(1,128)S(1)}, f32[10,1,258]{2,1,0:T(1,128)S(1)}, u32[]{:S(2)}, u32[]{:S(2)}) collective-permute-start(f32[10,1,258]{2,1,0:T(1,128)S(1)} %get-tuple-element.19), channel_id=1, source_target_pairs={{1,0},{2,1},{3,2},{4,3},{5,4},{6,5},{7,6},{8,7},{9,8},{10,9},{11,1... | collective-permute-start | bytes 30968 | tf_op jit(solution)/shard_map/ppermute | solution.py:24
  127.9 16.5 %collective-permute-start.16 = (f32[10,1,258]{2,1,0:T(1,128)S(1)}, f32[10,1,258]{2,1,0:T(1,128)S(1)}, u32[]{:S(2)}, u32[]{:S(2)}) collective-permute-start(f32[10,1,258]{2,1,0:T(1,128)S(1)} %get-tuple-element.18), channel_id=1, source_target_pairs={{0,1},{1,2},{2,3},{3,4},{4,5},{5,6},{6,7},{7,8},{8,9},{9,10},{10,1... | collective-permute-start | bytes 30968 | tf_op jit(solution)/shard_map/ppermute | solution.py:22
  144.9 5.3 %collective-permute-start.31 = (f32[8,16,1]{2,1,0:T(8,128)S(1)}, f32[8,16,1]{2,1,0:T(8,128)S(1)}, u32[]{:S(2)}, u32[]{:S(2)}) collective-permute-start(f32[8,16,1]{2,1,0:T(8,128)S(1)} %get-tuple-element.37), channel_id=1, source_target_pairs={{128,0},{256,128},{384,256},{129,1},{257,129},{385,257},{130,2},{2... | collective-permute-start | bytes 1544 | tf_op jit(solution)/shard_map/ppermute | solution.py:24
  147.0 5.0 %collective-permute-start.30 = (f32[8,16,1]{2,1,0:T(8,128)S(1)}, f32[8,16,1]{2,1,0:T(8,128)S(1)}, u32[]{:S(2)}, u32[]{:S(2)}) collective-permute-start(f32[8,16,1]{2,1,0:T(8,128)S(1)} %get-tuple-element.36), channel_id=1, source_target_pairs={{0,128},{128,256},{256,384},{1,129},{129,257},{257,385},{2,130},{1... | collective-permute-start | bytes 1544 | tf_op jit(solution)/shard_map/ppermute | solution.py:22
  152.1 7.7 %collective-permute-start.33 = (f32[1,16,258]{2,1,0:T(8,128)S(1)}, f32[1,16,258]{2,1,0:T(8,128)S(1)}, u32[]{:S(2)}, u32[]{:S(2)}) collective-permute-start(f32[1,16,258]{2,1,0:T(8,128)S(1)} %get-tuple-element.27), channel_id=1, source_target_pairs={{16,0},{32,16},{48,32},{64,48},{80,64},{96,80},{112,96},{17,1},{33... | collective-permute-start | bytes 49544 | tf_op jit(solution)/shard_map/ppermute | solution.py:24
  154.1 6.7 %collective-permute-start.32 = (f32[1,16,258]{2,1,0:T(8,128)S(1)}, f32[1,16,258]{2,1,0:T(8,128)S(1)}, u32[]{:S(2)}, u32[]{:S(2)}) collective-permute-start(f32[1,16,258]{2,1,0:T(8,128)S(1)} %get-tuple-element.26), channel_id=1, source_target_pairs={{0,16},{16,32},{32,48},{48,64},{64,80},{80,96},{96,112},{1,17},{17... | collective-permute-start | bytes 49544 | tf_op jit(solution)/shard_map/ppermute | solution.py:22
  160.9 7.4 %collective-permute-start.35 = (f32[10,1,258]{2,1,0:T(1,128)S(1)}, f32[10,1,258]{2,1,0:T(1,128)S(1)}, u32[]{:S(2)}, u32[]{:S(2)}) collective-permute-start(f32[10,1,258]{2,1,0:T(1,128)S(1)} %get-tuple-element.17), channel_id=1, source_target_pairs={{1,0},{2,1},{3,2},{4,3},{5,4},{6,5},{7,6},{8,7},{9,8},{10,9},{11,1... | collective-permute-start | bytes 30968 | tf_op jit(solution)/shard_map/ppermute | solution.py:24
  162.8 6.3 %collective-permute-start.34 = (f32[10,1,258]{2,1,0:T(1,128)S(1)}, f32[10,1,258]{2,1,0:T(1,128)S(1)}, u32[]{:S(2)}, u32[]{:S(2)}) collective-permute-start(f32[10,1,258]{2,1,0:T(1,128)S(1)} %get-tuple-element.16), channel_id=1, source_target_pairs={{0,1},{1,2},{2,3},{3,4},{4,5},{5,6},{6,7},{7,8},{8,9},{9,10},{10,1... | collective-permute-start | bytes 30968 | tf_op jit(solution)/shard_map/ppermute | solution.py:22
  183.5 10.8 %collective-permute-start.43 = (f32[4,8,1]{2,1,0:T(8,128)S(1)}, f32[4,8,1]{2,1,0:T(8,128)S(1)}, u32[]{:S(2)}, u32[]{:S(2)}) collective-permute-start(f32[4,8,1]{2,1,0:T(8,128)S(1)} %get-tuple-element.57), channel_id=1, source_target_pairs={{128,0},{256,128},{384,256},{129,1},{257,129},{385,257},{130,2},{2... | collective-permute-start | bytes 392 | tf_op jit(solution)/shard_map/ppermute | solution.py:24
  185.4 8.9 %collective-permute-start.42 = (f32[4,8,1]{2,1,0:T(8,128)S(1)}, f32[4,8,1]{2,1,0:T(8,128)S(1)}, u32[]{:S(2)}, u32[]{:S(2)}) collective-permute-start(f32[4,8,1]{2,1,0:T(8,128)S(1)} %get-tuple-element.56), channel_id=1, source_target_pairs={{0,128},{128,256},{256,384},{1,129},{129,257},{257,385},{2,130},{1... | collective-permute-start | bytes 392 | tf_op jit(solution)/shard_map/ppermute | solution.py:22
  189.1 15.9 %collective-permute-start.37 = (f32[8,16,1]{2,1,0:T(8,128)S(1)}, f32[8,16,1]{2,1,0:T(8,128)S(1)}, u32[]{:S(2)}, u32[]{:S(2)}) collective-permute-start(f32[8,16,1]{2,1,0:T(8,128)S(1)} %get-tuple-element.35), channel_id=1, source_target_pairs={{128,0},{256,128},{384,256},{129,1},{257,129},{385,257},{130,2},{2... | collective-permute-start | bytes 1544 | tf_op jit(solution)/shard_map/ppermute | solution.py:24
  191.0 14.0 %collective-permute-start.36 = (f32[8,16,1]{2,1,0:T(8,128)S(1)}, f32[8,16,1]{2,1,0:T(8,128)S(1)}, u32[]{:S(2)}, u32[]{:S(2)}) collective-permute-start(f32[8,16,1]{2,1,0:T(8,128)S(1)} %get-tuple-element.34), channel_id=1, source_target_pairs={{0,128},{128,256},{256,384},{1,129},{129,257},{257,385},{2,130},{1... | collective-permute-start | bytes 1544 | tf_op jit(solution)/shard_map/ppermute | solution.py:22
  194.4 18.3 %collective-permute-start.45 = (f32[1,8,130]{2,1,0:T(8,128)S(1)}, f32[1,8,130]{2,1,0:T(8,128)S(1)}, u32[]{:S(2)}, u32[]{:S(2)}) collective-permute-start(f32[1,8,130]{2,1,0:T(8,128)S(1)} %get-tuple-element.51), channel_id=1, source_target_pairs={{16,0},{32,16},{48,32},{64,48},{80,64},{96,80},{112,96},{17,1},{33... | collective-permute-start | bytes 12488 | tf_op jit(solution)/shard_map/ppermute | solution.py:24
  196.9 15.9 %collective-permute-start.44 = (f32[1,8,130]{2,1,0:T(8,128)S(1)}, f32[1,8,130]{2,1,0:T(8,128)S(1)}, u32[]{:S(2)}, u32[]{:S(2)}) collective-permute-start(f32[1,8,130]{2,1,0:T(8,128)S(1)} %get-tuple-element.50), channel_id=1, source_target_pairs={{0,16},{16,32},{32,48},{48,64},{64,80},{80,96},{96,112},{1,17},{17... | collective-permute-start | bytes 12488 | tf_op jit(solution)/shard_map/ppermute | solution.py:22
  205.1 15.8 %collective-permute-start.39 = (f32[1,16,258]{2,1,0:T(8,128)S(1)}, f32[1,16,258]{2,1,0:T(8,128)S(1)}, u32[]{:S(2)}, u32[]{:S(2)}) collective-permute-start(f32[1,16,258]{2,1,0:T(8,128)S(1)} %get-tuple-element.25), channel_id=1, source_target_pairs={{16,0},{32,16},{48,32},{64,48},{80,64},{96,80},{112,96},{17,1},{33... | collective-permute-start | bytes 49544 | tf_op jit(solution)/shard_map/ppermute | solution.py:24
  207.0 13.9 %collective-permute-start.38 = (f32[1,16,258]{2,1,0:T(8,128)S(1)}, f32[1,16,258]{2,1,0:T(8,128)S(1)}, u32[]{:S(2)}, u32[]{:S(2)}) collective-permute-start(f32[1,16,258]{2,1,0:T(8,128)S(1)} %get-tuple-element.24), channel_id=1, source_target_pairs={{0,16},{16,32},{32,48},{48,64},{64,80},{80,96},{96,112},{1,17},{17... | collective-permute-start | bytes 49544 | tf_op jit(solution)/shard_map/ppermute | solution.py:22
  212.9 15.5 %collective-permute-start.47 = (f32[6,1,130]{2,1,0:T(1,128)S(1)}, f32[6,1,130]{2,1,0:T(1,128)S(1)}, u32[]{:S(2)}, u32[]{:S(2)}) collective-permute-start(f32[6,1,130]{2,1,0:T(1,128)S(1)} %get-tuple-element.45), channel_id=1, source_target_pairs={{1,0},{2,1},{3,2},{4,3},{5,4},{6,5},{7,6},{8,7},{9,8},{10,9},{11,1... | collective-permute-start | bytes 9368 | tf_op jit(solution)/shard_map/ppermute | solution.py:24
  214.8 13.6 %collective-permute-start.46 = (f32[6,1,130]{2,1,0:T(1,128)S(1)}, f32[6,1,130]{2,1,0:T(1,128)S(1)}, u32[]{:S(2)}, u32[]{:S(2)}) collective-permute-start(f32[6,1,130]{2,1,0:T(1,128)S(1)} %get-tuple-element.44), channel_id=1, source_target_pairs={{0,1},{1,2},{2,3},{3,4},{4,5},{5,6},{6,7},{7,8},{8,9},{9,10},{10,1... | collective-permute-start | bytes 9368 | tf_op jit(solution)/shard_map/ppermute | solution.py:22
  221.0 18.4 %collective-permute-start.41 = (f32[10,1,258]{2,1,0:T(1,128)S(1)}, f32[10,1,258]{2,1,0:T(1,128)S(1)}, u32[]{:S(2)}, u32[]{:S(2)}) collective-permute-start(f32[10,1,258]{2,1,0:T(1,128)S(1)} %get-tuple-element.15), channel_id=1, source_target_pairs={{1,0},{2,1},{3,2},{4,3},{5,4},{6,5},{7,6},{8,7},{9,8},{10,9},{11,1... | collective-permute-start | bytes 30968 | tf_op jit(solution)/shard_map/ppermute | solution.py:24
  222.9 16.5 %collective-permute-start.40 = (f32[10,1,258]{2,1,0:T(1,128)S(1)}, f32[10,1,258]{2,1,0:T(1,128)S(1)}, u32[]{:S(2)}, u32[]{:S(2)}) collective-permute-start(f32[10,1,258]{2,1,0:T(1,128)S(1)} %get-tuple-element.14), channel_id=1, source_target_pairs={{0,1},{1,2},{2,3},{3,4},{4,5},{5,6},{6,7},{7,8},{8,9},{9,10},{10,1... | collective-permute-start | bytes 30968 | tf_op jit(solution)/shard_map/ppermute | solution.py:22
  (3 other events, 143.8 us)
where the time goes:
time: 242 us; the launch traced here: 241 us
  starting transfers between devices  165 us (68%)
  local copies, waits for them, and re-layouts  54.1 us (22%)
  other arithmetic  16.6 us (7%)
  waiting for transfers between devices  3.73 us (2%)
    ppermute x24, starting transfers between devices, extended(): lax.ppermute(tail, axis, [(i, (i + 1) % count) for i in range(ends)])  114 us
    ppermute x24, starting transfers between devices, extended(): lax.ppermute(head, axis, [((i + 1) % count, i) for i in range(ends)])  51.5 us
    reshape x3, local copies, waits for them, and re-layouts, block_mean(): field.reshape(sizea // 2, 2, sizeb // 2, 2, sizec // 2, 2)  30.1 us
    reshape x2, local copies, waits for them, and re-layouts, prolong(): return spread.reshape(2 * sizea, 2 * sizeb, 2 * sizec)  13.9 us
    reduce_sum x3, other arithmetic, block_mean(): field.reshape(sizea // 2, 2, sizeb // 2, 2, sizec // 2, 2)  12.1 us
    broadcast_in_dim x2, local copies, waits for them, and re-layouts, prolong(): jnp.broadcast_to(coarse[:, None, :, None, :, None], (sizea, 2, sizeb, 2,...  7.8 us
  transfers between devices with their start and end apart: 48, of which 3 were waited for; matrix products, arithmetic and copies ran while one was open for 22% of the time, Pallas kernels for 0%

commit v1 on v0

v1 whole, which is shorter than its diff:
```python
import functools

import jax
import jax.numpy as jnp
from jax import lax
from jax.experimental import pallas as pl
from jax.experimental.pallas import tpu as pltpu
from jax.sharding import PartitionSpec as P

MESH = pl.DeviceIdType.MESH
F32 = jnp.float32

NX, NY, NZ = 8, 16, 256
CX = NX // 2
ROWS = NX * NY
HALVES = (0, 1)
TILES = (0, 1)

FIRST_RATE = 0.8
KEEP = 60.0 / 41.0
FRESH = 40.0 / 41.0

FACES = (("gx", -1), ("gx", 1), ("gy", -1), ("gy", 1), ("grp", -1), ("grp", 1))
SIZES = (9, 9, 5, 5, 2, 2)
ROUND_SIZES = (SIZES, (5, 5, 3, 3, 1, 1), (4, 4, 2, 2, 1, 1), (5, 5, 3, 3, 1, 1))
OFFSETS = (0, 9, 18, 23, 28, 30)
SLOTS = 32
SECOND = (5, 5, 3, 3, 1, 1)


def iota(shape, dim):
    return lax.broadcasted_iota(jnp.int32, shape, dim)


def kernel(source_hbm, cond_hbm, field_hbm, out_hbm, source, half_cond, field, first, out, ky_lo, ky_hi, kz_lo, kz_hi,
           diag, inverse, partial, coarse_half, cky_lo, cky_hi, ckz_lo, ckz_hi, coarse_diag, coarse_inverse, coarse_first,
           faces, gains, sent, received, in_sem, out_sem, send_sem, recv_sem):
    sub, lane = iota((2, 8, 128), 1), iota((2, 8, 128), 2)
    sub2, lane2 = iota((8, 128), 0), iota((8, 128), 1)
    even_sub, even_lane = sub % 2 == 0, lane % 2 == 0
    even_sub2, even_lane2 = sub2 % 2 == 0, lane2 % 2 == 0
    zero = jnp.zeros((1, 8, 128), F32)
    zero2 = jnp.zeros((2, 8, 128), F32)

    place = {name: lax.axis_index(name) for name in ("grp", "gx", "gy")}
    size = {name: lax.axis_size(name) for name in ("grp", "gx", "gy")}
    present = []
    for name, step in FACES:
        present.append(place[name] > 0 if step < 0 else place[name] < size[name] - 1)

    def plane(ref, half, x):
        return ref[half, NY * x : NY * (x + 1), :].reshape(2, 8, 128)

    def put(ref, half, x, value):
        ref[half, NY * x : NY * (x + 1), :] = value.reshape(16, 128)

    def y_lower(p, width=1):
        rolled = pltpu.roll(p, width, 1)
        return jnp.where(sub < width, jnp.concatenate([zero, rolled[:1]], axis=0), rolled)

    def y_upper(p, width=1):
        rolled = pltpu.roll(p, 8 - width, 1)
        return jnp.where(sub >= 8 - width, jnp.concatenate([rolled[1:], zero], axis=0), rolled)

    def z_lower(p0, p1, width=1):
        r0, r1 = pltpu.roll(p0, width, 2), pltpu.roll(p1, width, 2)
        return jnp.where(lane < width, 0.0, r0), jnp.where(lane < width, r0, r1)

    def z_upper(p0, p1, width=1):
        r0, r1 = pltpu.roll(p0, 128 - width, 2), pltpu.roll(p1, 128 - width, 2)
        return jnp.where(lane >= 128 - width, r1, r0), jnp.where(lane >= 128 - width, 0.0, r1)

    def neighbour_sum(ref, half_ref, kyl, kyh, kzl, kzh, x, count, width):
        p = [plane(ref, h, x) for h in HALVES]
        zl, zh = z_lower(p[0], p[1], width), z_upper(p[0], p[1], width)
        here = [plane(half_ref, h, x) for h in HALVES]
        total = []
        for h in HALVES:
            s = plane(kyl, h, x) * y_lower(p[h], width) + plane(kyh, h, x) * y_upper(p[h], width)
            s = s + (plane(kzl, h, x) * zl[h] + plane(kzh, h, x) * zh[h])
            if x > 0:
                s = s + (here[h] + plane(half_ref, h, x - 1)) * plane(ref, h, x - 1)
            if x < count - 1:
                s = s + (here[h] + plane(half_ref, h, x + 1)) * plane(ref, h, x + 1)
            total.append(s)
        return total

    def fine_neighbours(ref, x):
        return neighbour_sum(ref, half_cond, ky_lo, ky_hi, kz_lo, kz_hi, x, NX, 1)

    def coarse_neighbours(ref, x):
        return neighbour_sum(ref, coarse_half, cky_lo, cky_hi, ckz_lo, ckz_hi, x, CX, 2)

    def coefficients(ref, kyl, kyh, kzl, kzh, diag_ref, x, count, width):
        p = [plane(ref, h, x) for h in HALVES]
        zl, zh = z_lower(p[0], p[1], width), z_upper(p[0], p[1], width)
        for h in HALVES:
            yl, yh = y_lower(p[h], width), y_upper(p[h], width)
            put(kyl, h, x, p[h] + yl)
            put(kyh, h, x, p[h] + yh)
            put(kzl, h, x, p[h] + zl[h])
            put(kzh, h, x, p[h] + zh[h])
            s = 6.0 * p[h] + ((yl + yh) + (zl[h] + zh[h]))
            if x > 0:
                s = s + plane(ref, h, x - 1)
            if x < count - 1:
                s = s + plane(ref, h, x + 1)
            put(diag_ref, h, x, s)

    def restrict(lower, upper):
        s = lower + upper
        s = s + jnp.where(even_sub, pltpu.roll(s, 7, 1), pltpu.roll(s, 1, 1))
        s = s + jnp.where(even_lane, pltpu.roll(s, 127, 2), pltpu.roll(s, 1, 2))
        return 0.125 * s

    def message(store, turn, face):
        return store.at[turn, pl.ds(OFFSETS[face], ROUND_SIZES[turn][face])]

    def slot(face, index):
        return OFFSETS[face] + index

    def pack_fine(ref, turn, second):
        for face, x in ((0, 0), (1, NX - 1)):
            base = slot(face, SECOND[face] if second else 0)
            for h in HALVES:
                sent[turn, base + 2 * h : base + 2 * h + 2] = plane(ref, h, x)
        for face, row in ((2, 0), (3, NY - 1)):
            base = slot(face, SECOND[face] if second else 0)
            for h in HALVES:
                sent[turn, base + h] = ref[h, pl.ds(row, NX, stride=NY), :]
        columns = []
        for face, h, source_lane in ((4, 0, 0), (5, 1, 127)):
            packed = jnp.zeros((8, 128), F32)
            for x in range(NX):
                p = plane(ref, h, x)
                for t in TILES:
                    m = 2 * x + t
                    packed = jnp.where(lane2 == m, pltpu.roll(p[t], (m - source_lane) % 128, 1), packed)
            columns.append(packed)
        return columns

    def pack_coarse(ref, turn, columns):
        for face, x in ((0, 0), (1, CX - 1)):
            p = [plane(ref, h, x) for h in HALVES]
            sent[turn, slot(face, 4)] = jnp.where(
                even_sub2, jnp.where(even_lane2, p[0][0], p[1][0]), jnp.where(even_lane2, p[0][1], p[1][1]))
        for face, row in ((2, 0), (3, NY - 1)):
            for h in HALVES:
                sent[turn, slot(face, 2), CX * h : CX * (h + 1), :] = ref[h, pl.ds(row, CX, stride=NY), :]
        packed_columns = []
        for packed, (face, h, source_lane) in zip(columns, ((4, 0, 0), (5, 1, 127))):
            for x in range(CX):
                p = plane(ref, h, x)
                for t in TILES:
                    m = 16 + 2 * x + t
                    packed = jnp.where(lane2 == m, pltpu.roll(p[t], (m - source_lane) % 128, 1), packed)
            packed_columns.append(packed)
        return packed_columns

    def store_columns(turn, columns, index):
        for face, packed in zip((4, 5), columns):
            sent[turn, slot(face, index)] = packed

    def spread_fine(q, half, x):
        rows = jnp.concatenate([
            jnp.broadcast_to(q[slot(2, half), x : x + 1, :], (8, 128))[None],
            jnp.broadcast_to(q[slot(3, half), x : x + 1, :], (8, 128))[None],
        ], axis=0)
        tile = iota((2, 8, 128), 0)
        out_ = jnp.where(sub == 7 * tile, rows, 0.0)
        column = q[slot(4 + half, 0)]
        columns = jnp.concatenate([
            jnp.broadcast_to(column[:, 2 * x + t : 2 * x + t + 1], (8, 128))[None] for t in TILES], axis=0)
        out_ = out_ + jnp.where(lane == 127 * half, columns, 0.0)
        if x == 0:
            out_ = out_ + q[slot(0, 2 * half) : slot(0, 2 * half) + 2]
        if x == NX - 1:
            out_ = out_ + q[slot(1, 2 * half) : slot(1, 2 * half) + 2]
        return out_

    def spread_coarse_plane(q, face):
        packed = q[slot(face, 4)]
        by_half = (jnp.where(even_lane2, packed, pltpu.roll(packed, 1, 1)),
                   jnp.where(even_lane2, pltpu.roll(packed, 127, 1), packed))
        return [jnp.concatenate([jnp.where(even_sub2, p, pltpu.roll(p, 1, 0))[None],
                                 jnp.where(even_sub2, pltpu.roll(p, 7, 0), p)[None]], axis=0) for p in by_half]

    def spread_coarse(q, half, x, planes):
        rows = jnp.concatenate([
            jnp.broadcast_to(q[slot(face, 2), CX * half + x : CX * half + x + 1, :], (8, 128))[None] for face in (2, 3)],
            axis=0)
        tile = iota((2, 8, 128), 0)
        out_ = jnp.where((sub // 2) == 3 * tile, rows, 0.0)
        column = q[slot(4 + half, 0)]
        columns = jnp.concatenate([
            jnp.broadcast_to(column[:, 16 + 2 * x + t : 17 + 2 * x + t], (8, 128))[None] for t in TILES], axis=0)
        out_ = out_ + jnp.where((lane // 2) == 63 * half, columns, 0.0)
        if x == 0:
            out_ = out_ + planes[0][half]
        if x == CX - 1:
            out_ = out_ + planes[1][half]
        return out_

    def peer(face):
        name, step = FACES[face]
        return {name: place[name] + step}

    def copy(turn, face):
        return pltpu.make_async_remote_copy(
            src_ref=message(sent, turn, face),
            dst_ref=message(received, turn, face ^ 1),
            send_sem=send_sem.at[turn, face],
            recv_sem=recv_sem.at[turn, face ^ 1],
            device_id=peer(face),
            device_id_type=MESH,
        )

    def arrival(turn, face):
        return pltpu.make_async_remote_copy(
            src_ref=message(sent, turn, face),
            dst_ref=message(received, turn, face),
            send_sem=send_sem.at[turn, face],
            recv_sem=recv_sem.at[turn, face],
            device_id=peer(face),
            device_id_type=MESH,
        )

    ORDER = (1, 0, 3, 2, 5, 4)

    def send(turn):
        for face in ORDER:
            @pl.when(present[face])
            def _():
                copy(turn, face).start()

    def wait(turn):
        for face in (5, 4, 3, 2, 1, 0):
            @pl.when(present[face])
            def _():
                arrival(turn, face).wait_recv()

    barrier = pltpu.get_barrier_semaphore()
    for face in range(6):
        @pl.when(present[face])
        def _():
            pl.semaphore_signal(barrier, inc=1, device_id=peer(face), device_id_type=MESH)

    loads = []
    for index, (hbm, ref) in enumerate(((cond_hbm, half_cond), (field_hbm, field), (source_hbm, source))):
        pair = []
        for h in HALVES:
            load = pltpu.make_async_copy(hbm.at[:, pl.ds(128 * h, 128)], ref.at[h], in_sem.at[index, h])
            load.start()
            pair.append(load)
        loads.append(pair)

    for face in range(6):
        @pl.when(jnp.logical_not(present[face]))
        def _():
            for turn in range(4):
                count = ROUND_SIZES[turn][face]
                received[turn, OFFSETS[face] : OFFSETS[face] + count] = jnp.zeros((count, 8, 128), F32)

    for load in loads[0]:
        load.wait()
    for x in range(NX):
        for h in HALVES:
            put(half_cond, h, x, 0.5 * plane(half_cond, h, x))
    for x in range(CX):
        for h in HALVES:
            put(coarse_half, h, x, restrict(plane(half_cond, h, 2 * x), plane(half_cond, h, 2 * x + 1)))
    store_columns(0, pack_coarse(coarse_half, 0, pack_fine(half_cond, 0, False)), 0)
    for load in loads[1]:
        load.wait()
    store_columns(0, pack_fine(field, 0, True), 1)

    pl.semaphore_wait(barrier, sum(p.astype(jnp.int32) for p in present))
    send(0)

    for x in range(NX):
        coefficients(half_cond, ky_lo, ky_hi, kz_lo, kz_hi, diag, x, NX, 1)
    for x in range(CX):
        coefficients(coarse_half, cky_lo, cky_hi, ckz_lo, ckz_hi, coarse_diag, x, CX, 2)
    for load in loads[2]:
        load.wait()

    def residual_part():
        for x in range(NX):
            total = fine_neighbours(field, x)
            for h in HALVES:
                put(partial, h, x, plane(source, h, x) - plane(diag, h, x) * plane(field, h, x) + total[h])

    residual_part()

    wait(0)
    for face in range(6):
        base, own, two = OFFSETS[face], SECOND[face], SECOND[face] - 1
        for i in range(own):
            gain = sent[0, base + i] + received[0, base + i]
            gains[base + i] = gain
        for i in range(SIZES[face] - own):
            faces[base + i] = (gains[base + i] * received[0, base + own + i]
                               - received[0, base + i] * sent[0, base + own + i])

    jplanes = (spread_coarse_plane(received.at[0], 0), spread_coarse_plane(received.at[0], 1))
    for x in range(CX):
        for h in HALVES:
            total = plane(coarse_diag, h, x) + spread_coarse(received.at[0], h, x, jplanes)
            put(coarse_inverse, h, x, 1.0 / total)
    for x in range(NX):
        for h in HALVES:
            total = plane(diag, h, x) + spread_fine(received.at[0], h, x)
            put(diag, h, x, total)
            put(inverse, h, x, 1.0 / total)

    for iteration in range(2):
        turn = 2 * iteration + 1
        if iteration > 0:
            wait(2)
            for face in range(6):
                base = OFFSETS[face]
                for i in range(ROUND_SIZES[2][face]):
                    faces[base + i] = gains[base + i] * received[2, base + i]
        for x in range(CX):
            for h in HALVES:
                pair = []
                for fx in (2 * x, 2 * x + 1):
                    r = plane(partial, h, fx) + spread_fine(faces, h, fx)
                    put(first, h, fx, FIRST_RATE * plane(inverse, h, fx) * r)
                    pair.append(r)
                put(coarse_first, h, x, 4.0 * FIRST_RATE * plane(coarse_inverse, h, x) * restrict(*pair))
        store_columns(turn, pack_coarse(coarse_first, turn, pack_fine(first, turn, False)), 0)
        send(turn)

        for x in range(CX):
            total = coarse_neighbours(coarse_first, x)
            coarse = [KEEP * plane(coarse_first, h, x) + FRESH * plane(coarse_inverse, h, x) * total[h] for h in HALVES]
            for fx in (2 * x, 2 * x + 1):
                total = fine_neighbours(first, fx)
                for h in HALVES:
                    fine = KEEP * plane(first, h, fx) + FRESH * plane(inverse, h, fx) * total[h]
                    put(partial, h, fx, plane(field, h, fx) + fine + coarse[h])

        wait(turn)
        for face in range(6):
            base = OFFSETS[face]
            for i in range(ROUND_SIZES[turn][face]):
                faces[base + i] = (FRESH * gains[base + i]) * received[turn, base + i]
        planes = (spread_coarse_plane(faces, 0), spread_coarse_plane(faces, 1))
        target = out if iteration == 1 else field
        for x in range(CX):
            for h in HALVES:
                coarse = plane(coarse_inverse, h, x) * spread_coarse(faces, h, x, planes)
                for fx in (2 * x, 2 * x + 1):
                    fine = plane(inverse, h, fx) * spread_fine(faces, h, fx)
                    put(target, h, fx, plane(partial, h, fx) + fine + coarse)
        if iteration == 0:
            store_columns(2, pack_fine(field, 2, False), 0)
            send(2)
            residual_part()

    stores = [pltpu.make_async_copy(out.at[h], out_hbm.at[:, pl.ds(128 * h, 128)], out_sem.at[h]) for h in HALVES]
    for store in stores:
        store.start()
    for turn in range(4):
        for face in range(6):
            @pl.when(present[face])
            def _():
                copy(turn, face).wait_send()
    for store in stores:
        store.wait()


def block(source_term, conductivity, initial_field):
    def fine():
        return pltpu.VMEM((2, ROWS, 128), F32)

    def coarse():
        return pltpu.VMEM((2, CX * NY, 128), F32)

    hbm = pl.BlockSpec(memory_space=pltpu.HBM)
    result = pl.pallas_call(
        kernel,
        out_shape=jax.ShapeDtypeStruct((ROWS, NZ), F32),
        in_specs=[hbm] * 3,
        out_specs=hbm,
        scratch_shapes=[
            *(fine() for _ in range(12)),
            *(coarse() for _ in range(8)),
            pltpu.VMEM((SLOTS, 8, 128), F32),
            pltpu.VMEM((SLOTS, 8, 128), F32),
            pltpu.VMEM((4, SLOTS, 8, 128), F32),
            pltpu.VMEM((4, SLOTS, 8, 128), F32),
            pltpu.SemaphoreType.DMA((3, 2)),
            pltpu.SemaphoreType.DMA((2,)),
            pltpu.SemaphoreType.DMA((4, 6)),
            pltpu.SemaphoreType.DMA((4, 6)),
        ],
        compiler_params=pltpu.CompilerParams(collective_id=0, has_side_effects=True),
    )(*(a.reshape(ROWS, NZ) for a in (source_term, conductivity, initial_field)))
    return result.reshape(NX, NY, NZ)


def solution(mesh):
    spec = P("gx", "gy", "grp")
    return jax.shard_map(block, mesh=mesh, in_specs=(spec,) * 3, out_specs=spec, check_vma=False)
```

time: 242 us -> 25.5 us (0.11)
  the two profiles are of different devices: /device:TPU:219 before, /device:TPU:213 now
where the time goes in v1:
time: 25.5 us; the launch traced here: 25.3 us
  Pallas kernels  23.8 us (93%)
  local copies, waits for them, and re-layouts  1.57 us (6%)
    pallas_call x1, Pallas kernels, block(): pl.pallas_call(kernel, out_shape=jax.ShapeDtypeStruct((ROWS, NZ), F32), i...  23.8 us
    unnamed x1, local copies, waits for them, and re-layouts  1.57 us

profile of v1, /device:TPU:213, one launch (start us, length us, event | category | flops | bytes accessed | tf_op | source)
XLA Modules:
  0.0 25.3 jit_solution(5432328930828490052)
XLA Ops:
  0.0 23.8 %shard_map.37 = f32[128,256]{1,0:T(8,128)} custom-call(f32[128,256]{1,0:T(8,128)} %bitcast.5, f32[128,256]{1,0:T(8,128)} %bitcast.6, f32[128,256]{1,0:T(8,128)} %bitcast.7), custom_call_target="tpu_custom_call" | custom-call | tf_op jit(solution)/shard_map/pallas_call | solution.py:382
  23.8 1.6 %copy.5 = f32[8,16,256]{2,1,0:T(8,128)} copy(f32[8,16,256]{2,1,0:T(8,128)} %bitcast.4) | data formatting | bytes 262144

commit v2 on v1

--- a/solution.py
+++ b/solution.py
@@ -32,9 +32,9 @@
     return lax.broadcasted_iota(jnp.int32, shape, dim)
 
 
-def kernel(source_hbm, cond_hbm, field_hbm, out_hbm, source, half_cond, field, first, out, ky_lo, ky_hi, kz_lo, kz_hi,
+def kernel(source_hbm, cond_hbm, field_hbm, out, source, half_cond, field, first, ky_lo, ky_hi, kz_lo, kz_hi,
            diag, inverse, partial, coarse_half, cky_lo, cky_hi, ckz_lo, ckz_hi, coarse_diag, coarse_inverse, coarse_first,
-           faces, gains, sent, received, in_sem, out_sem, send_sem, recv_sem):
+           faces, gains, sent, received, in_sem, send_sem, recv_sem):
     sub, lane = iota((2, 8, 128), 1), iota((2, 8, 128), 2)
     sub2, lane2 = iota((8, 128), 0), iota((8, 128), 1)
     even_sub, even_lane = sub % 2 == 0, lane % 2 == 0
@@ -347,28 +347,26 @@
             for i in range(ROUND_SIZES[turn][face]):
                 faces[base + i] = (FRESH * gains[base + i]) * received[turn, base + i]
         planes = (spread_coarse_plane(faces, 0), spread_coarse_plane(faces, 1))
-        target = out if iteration == 1 else field
         for x in range(CX):
             for h in HALVES:
                 coarse = plane(coarse_inverse, h, x) * spread_coarse(faces, h, x, planes)
                 for fx in (2 * x, 2 * x + 1):
                     fine = plane(inverse, h, fx) * spread_fine(faces, h, fx)
-                    put(target, h, fx, plane(partial, h, fx) + fine + coarse)
+                    value = plane(partial, h, fx) + fine + coarse
+                    if iteration == 0:
+                        put(field, h, fx, value)
+                    else:
+                        out[NY * fx : NY * (fx + 1), 128 * h : 128 * (h + 1)] = value.reshape(16, 128)
         if iteration == 0:
             store_columns(2, pack_fine(field, 2, False), 0)
             send(2)
             residual_part()
 
-    stores = [pltpu.make_async_copy(out.at[h], out_hbm.at[:, pl.ds(128 * h, 128)], out_sem.at[h]) for h in HALVES]
-    for store in stores:
-        store.start()
     for turn in range(4):
         for face in range(6):
             @pl.when(present[face])
             def _():
                 copy(turn, face).wait_send()
-    for store in stores:
-        store.wait()
 
 
 def block(source_term, conductivity, initial_field):
@@ -381,18 +379,17 @@
     hbm = pl.BlockSpec(memory_space=pltpu.HBM)
     result = pl.pallas_call(
         kernel,
-        out_shape=jax.ShapeDtypeStruct((ROWS, NZ), F32),
+        out_shape=pltpu.VMEM((ROWS, NZ), F32),
         in_specs=[hbm] * 3,
-        out_specs=hbm,
+        out_specs=pl.BlockSpec(memory_space=pltpu.VMEM),
         scratch_shapes=[
-            *(fine() for _ in range(12)),
+            *(fine() for _ in range(11)),
             *(coarse() for _ in range(8)),
             pltpu.VMEM((SLOTS, 8, 128), F32),
             pltpu.VMEM((SLOTS, 8, 128), F32),
             pltpu.VMEM((4, SLOTS, 8, 128), F32),
             pltpu.VMEM((4, SLOTS, 8, 128), F32),
             pltpu.SemaphoreType.DMA((3, 2)),
-            pltpu.SemaphoreType.DMA((2,)),
             pltpu.SemaphoreType.DMA((4, 6)),
             pltpu.SemaphoreType.DMA((4, 6)),
         ],

time: 25.5 us -> 23.9 us (0.937)
  local copies, waits for them, and re-layouts: 1.57 us -> 0.66 us
  Pallas kernels: 23.8 us -> 23.1 us
    unnamed x1, local copies, waits for them, and re-layouts: 1.57 us -> 0.66 us
    pallas_call x1, Pallas kernels: 23.8 us -> 23.1 us  [block(): pl.pallas_call(kernel, out_shape=pltpu.VMEM((ROWS, NZ), F32), in_specs=[h...]
where the time goes in v2:
time: 23.9 us; the launch traced here: 23.8 us
  Pallas kernels  23.1 us (97%)
  local copies, waits for them, and re-layouts  0.66 us (3%)
    pallas_call x1, Pallas kernels, block(): pl.pallas_call(kernel, out_shape=pltpu.VMEM((ROWS, NZ), F32), in_specs=[h...  23.1 us
    unnamed x1, local copies, waits for them, and re-layouts  0.66 us

profile of v2, /device:TPU:213, one launch (start us, length us, event | category | flops | bytes accessed | tf_op | source)
XLA Modules:
  0.0 23.8 jit_solution(7830469942245178682)
XLA Ops:
  0.0 23.1 %shard_map.37 = f32[128,256]{1,0:T(8,128)S(1)} custom-call(f32[128,256]{1,0:T(8,128)} %bitcast.5, f32[128,256]{1,0:T(8,128)} %bitcast.6, f32[128,256]{1,0:T(8,128)} %bitcast.7), custom_call_target="tpu_custom_call" | custom-call | tf_op jit(solution)/shard_map/pallas_call | solution.py:380
  23.1 0.7 %copy.5 = f32[8,16,256]{2,1,0:T(8,128)} copy(f32[8,16,256]{2,1,0:T(8,128)S(1)} %bitcast.4) | data formatting | bytes 262144

commit v3 on v2

v3 whole, which is shorter than its diff:
```python
import functools

import jax
import jax.numpy as jnp
from jax import lax
from jax.experimental import pallas as pl
from jax.experimental.pallas import tpu as pltpu
from jax.sharding import PartitionSpec as P

MESH = pl.DeviceIdType.MESH
F32 = jnp.float32

NX, NY, NZ = 8, 16, 256
CX = NX // 2
ROWS = NX * NY
HALVES = (0, 1)
TILES = (0, 1)

FIRST_RATE = 0.8
KEEP = 60.0 / 41.0
FRESH = 40.0 / 41.0

FACES = (("gx", -1), ("gx", 1), ("gy", -1), ("gy", 1), ("grp", -1), ("grp", 1))
BOTH = (5, 5, 3, 3, 1, 1)
FINE = (4, 4, 2, 2, 1, 1)
TURN_SIZES = (BOTH, FINE, BOTH, FINE, BOTH)
TURNS = len(TURN_SIZES)
OFFSETS = (0, 5, 10, 13, 16, 17)
SLOTS = 18
AXES = ((0, 1), (2, 3), (4, 5))


def iota(shape, dim):
    return lax.broadcasted_iota(jnp.int32, shape, dim)


def kernel(source_hbm, cond_hbm, field_hbm, out, source, half_cond, field, first, ky_lo, ky_hi, kz_lo, kz_hi,
           diag, inverse, partial, coarse_half, cky_lo, cky_hi, ckz_lo, ckz_hi, coarse_diag, coarse_inverse, coarse_first,
           faces, gains, scaled_gains, sent, received, in_sem, send_sem, recv_sem):
    sub, lane = iota((2, 8, 128), 1), iota((2, 8, 128), 2)
    sub2, lane2 = iota((8, 128), 0), iota((8, 128), 1)
    even_sub, even_lane = sub % 2 == 0, lane % 2 == 0
    even_sub2, even_lane2 = sub2 % 2 == 0, lane2 % 2 == 0
    zero = jnp.zeros((1, 8, 128), F32)
    tile = iota((2, 8, 128), 0)

    place = {name: lax.axis_index(name) for name in ("grp", "gx", "gy")}
    size = {name: lax.axis_size(name) for name in ("grp", "gx", "gy")}
    present = []
    for name, step in FACES:
        present.append(place[name] > 0 if step < 0 else place[name] < size[name] - 1)

    def plane(ref, half, x):
        return ref[half, NY * x : NY * (x + 1), :].reshape(2, 8, 128)

    def put(ref, half, x, value):
        ref[half, NY * x : NY * (x + 1), :] = value.reshape(16, 128)

    def y_lower(p, width=1):
        rolled = pltpu.roll(p, width, 1)
        return jnp.where(sub < width, jnp.concatenate([zero, rolled[:1]], axis=0), rolled)

    def y_upper(p, width=1):
        rolled = pltpu.roll(p, 8 - width, 1)
        return jnp.where(sub >= 8 - width, jnp.concatenate([rolled[1:], zero], axis=0), rolled)

    def z_lower(p0, p1, width=1):
        r0, r1 = pltpu.roll(p0, width, 2), pltpu.roll(p1, width, 2)
        return jnp.where(lane < width, 0.0, r0), jnp.where(lane < width, r0, r1)

    def z_upper(p0, p1, width=1):
        r0, r1 = pltpu.roll(p0, 128 - width, 2), pltpu.roll(p1, 128 - width, 2)
        return jnp.where(lane >= 128 - width, r1, r0), jnp.where(lane >= 128 - width, 0.0, r1)

    def neighbour_sum(ref, half_ref, kyl, kyh, kzl, kzh, x, count, width):
        p = [plane(ref, h, x) for h in HALVES]
        zl, zh = z_lower(p[0], p[1], width), z_upper(p[0], p[1], width)
        here = [plane(half_ref, h, x) for h in HALVES]
        total = []
        for h in HALVES:
            s = plane(kyl, h, x) * y_lower(p[h], width) + plane(kyh, h, x) * y_upper(p[h], width)
            s = s + (plane(kzl, h, x) * zl[h] + plane(kzh, h, x) * zh[h])
            if x > 0:
                s = s + (here[h] + plane(half_ref, h, x - 1)) * plane(ref, h, x - 1)
            if x < count - 1:
                s = s + (here[h] + plane(half_ref, h, x + 1)) * plane(ref, h, x + 1)
            total.append(s)
        return total

    def fine_neighbours(ref, x):
        return neighbour_sum(ref, half_cond, ky_lo, ky_hi, kz_lo, kz_hi, x, NX, 1)

    def coarse_neighbours(ref, x):
        return neighbour_sum(ref, coarse_half, cky_lo, cky_hi, ckz_lo, ckz_hi, x, CX, 2)

    def coefficients(ref, kyl, kyh, kzl, kzh, diag_ref, x, count, width):
        p = [plane(ref, h, x) for h in HALVES]
        zl, zh = z_lower(p[0], p[1], width), z_upper(p[0], p[1], width)
        for h in HALVES:
            yl, yh = y_lower(p[h], width), y_upper(p[h], width)
            put(kyl, h, x, p[h] + yl)
            put(kyh, h, x, p[h] + yh)
            put(kzl, h, x, p[h] + zl[h])
            put(kzh, h, x, p[h] + zh[h])
            s = 6.0 * p[h] + ((yl + yh) + (zl[h] + zh[h]))
            if x > 0:
                s = s + plane(ref, h, x - 1)
            if x < count - 1:
                s = s + plane(ref, h, x + 1)
            put(diag_ref, h, x, s)

    def restrict(lower, upper):
        s = lower + upper
        s = s + jnp.where(even_sub, pltpu.roll(s, 7, 1), pltpu.roll(s, 1, 1))
        s = s + jnp.where(even_lane, pltpu.roll(s, 127, 2), pltpu.roll(s, 1, 2))
        return 0.125 * s

    def slot(face, index):
        return OFFSETS[face] + index

    def message(store, turn, face):
        return store.at[turn, pl.ds(OFFSETS[face], TURN_SIZES[turn][face])]

    def pack_x(dest, fine, coarse=None):
        for face, x in ((0, 0), (1, NX - 1)):
            for h in HALVES:
                dest[slot(face, 2 * h) : slot(face, 2 * h) + 2] = plane(fine, h, x)
        if coarse is not None:
            for face, x in ((0, 0), (1, CX - 1)):
                p = [plane(coarse, h, x) for h in HALVES]
                dest[slot(face, 4)] = jnp.where(
                    even_sub2, jnp.where(even_lane2, p[0][0], p[1][0]), jnp.where(even_lane2, p[0][1], p[1][1]))

    def pack_y(dest, fine, coarse=None):
        for face, row in ((2, 0), (3, NY - 1)):
            for h in HALVES:
                dest[slot(face, h)] = fine[h, pl.ds(row, NX, stride=NY), :]
                if coarse is not None:
                    dest[slot(face, 2), CX * h : CX * (h + 1), :] = coarse[h, pl.ds(row, CX, stride=NY), :]

    def pack_z(dest, fine, coarse=None):
        for face, h, source_lane in ((4, 0, 0), (5, 1, 127)):
            packed = jnp.zeros((8, 128), F32)
            for ref, count, start in ((fine, NX, 0), (coarse, CX, 16)):
                if ref is None:
                    continue
                for x in range(count):
                    p = plane(ref, h, x)
                    for t in TILES:
                        m = start + 2 * x + t
                        packed = jnp.where(lane2 == m, pltpu.roll(p[t], (m - source_lane) % 128, 1), packed)
            dest[slot(face, 0)] = packed

    def two(a, b):
        return jnp.concatenate([a[None], b[None]], axis=0)

    def fine_z(q, half, x):
        column = q[slot(4 + half, 0)]
        return jnp.where(lane == 127 * half, two(*(
            jnp.broadcast_to(column[:, 2 * x + t : 2 * x + t + 1], (8, 128)) for t in TILES)), 0.0)

    def coarse_z(q, half, x):
        column = q[slot(4 + half, 0)]
        return jnp.where(lane // 2 == 63 * half, two(*(
            jnp.broadcast_to(column[:, 16 + 2 * x + t : 17 + 2 * x + t], (8, 128)) for t in TILES)), 0.0)

    def fine_xy(q, half, x):
        added = jnp.where(sub == 7 * tile, two(*(
            jnp.broadcast_to(q[slot(face, half), x : x + 1, :], (8, 128)) for face in (2, 3))), 0.0)
        if x == 0:
            added = added + q[slot(0, 2 * half) : slot(0, 2 * half) + 2]
        if x == NX - 1:
            added = added + q[slot(1, 2 * half) : slot(1, 2 * half) + 2]
        return added

    def coarse_plane(q, half, face):
        packed = q[slot(face, 4)]
        if half == 0:
            p = jnp.where(even_lane2, packed, pltpu.roll(packed, 1, 1))
        else:
            p = jnp.where(even_lane2, pltpu.roll(packed, 127, 1), packed)
        return two(jnp.where(even_sub2, p, pltpu.roll(p, 1, 0)), jnp.where(even_sub2, pltpu.roll(p, 7, 0), p))

    def coarse_xy(q, half, x):
        row = CX * half + x
        added = jnp.where(sub // 2 == 3 * tile, two(*(
            jnp.broadcast_to(q[slot(face, 2), row : row + 1, :], (8, 128)) for face in (2, 3))), 0.0)
        if x == 0:
            added = added + coarse_plane(q, half, 0)
        if x == CX - 1:
            added = added + coarse_plane(q, half, 1)
        return added

    def peer(face):
        name, step = FACES[face]
        return {name: place[name] + step}

    def copy(turn, face):
        return pltpu.make_async_remote_copy(
            src_ref=message(sent, turn, face),
            dst_ref=message(received, turn, face ^ 1),
            send_sem=send_sem.at[turn, face],
            recv_sem=recv_sem.at[turn, face ^ 1],
            device_id=peer(face),
            device_id_type=MESH,
        )

    def arrival(turn, face):
        return pltpu.make_async_remote_copy(
            src_ref=message(sent, turn, face),
            dst_ref=message(received, turn, face),
            send_sem=send_sem.at[turn, face],
            recv_sem=recv_sem.at[turn, face],
            device_id=peer(face),
            device_id_type=MESH,
        )

    def send(turn, axis):
        for face in reversed(AXES[axis]):
            @pl.when(present[face])
            def _():
                copy(turn, face).start()

    def wait(turn, axes):
        for axis in axes:
            for face in AXES[axis]:
                @pl.when(present[face])
                def _():
                    arrival(turn, face).wait_recv()

    def wait_sent(turn):
        for face in range(6):
            @pl.when(present[face])
            def _():
                copy(turn, face).wait_send()

    barrier = pltpu.get_barrier_semaphore()
    for face in range(6):
        @pl.when(present[face])
        def _():
            pl.semaphore_signal(barrier, inc=1, device_id=peer(face), device_id_type=MESH)

    loads = []
    for index, (hbm, ref) in enumerate(((cond_hbm, half_cond), (field_hbm, field), (source_hbm, source))):
        pair = []
        for h in HALVES:
            load = pltpu.make_async_copy(hbm.at[:, pl.ds(128 * h, 128)], ref.at[h], in_sem.at[index, h])
            load.start()
            pair.append(load)
        loads.append(pair)

    for face in range(6):
        @pl.when(jnp.logical_not(present[face]))
        def _():
            for turn in range(TURNS):
                count = TURN_SIZES[turn][face]
                received[turn, OFFSETS[face] : OFFSETS[face] + count] = jnp.zeros((count, 8, 128), F32)

    for load in loads[0]:
        load.wait()
    for x in range(NX):
        for h in HALVES:
            put(half_cond, h, x, 0.5 * plane(half_cond, h, x))
    for x in range(CX):
        for h in HALVES:
            put(coarse_half, h, x, restrict(plane(half_cond, h, 2 * x), plane(half_cond, h, 2 * x + 1)))
    for pack in (pack_x, pack_y, pack_z):
        pack(sent.at[0], half_cond, coarse_half)
    pl.semaphore_wait(barrier, sum(p.astype(jnp.int32) for p in present))
    for axis in range(3):
        send(0, axis)
    for load in loads[1]:
        load.wait()
    for axis, pack in enumerate((pack_x, pack_y, pack_z)):
        pack(sent.at[1], field)
        send(1, axis)

    for x in range(NX):
        coefficients(half_cond, ky_lo, ky_hi, kz_lo, kz_hi, diag, x, NX, 1)
    for x in range(CX):
        coefficients(coarse_half, cky_lo, cky_hi, ckz_lo, ckz_hi, coarse_diag, x, CX, 2)
    for load in loads[2]:
        load.wait()

    def residual_part():
        for x in range(NX):
            total = fine_neighbours(field, x)
            for h in HALVES:
                put(partial, h, x, plane(source, h, x) - plane(diag, h, x) * plane(field, h, x) + total[h])

    residual_part()

    wait(0, (2, 0, 1))
    for i in range(SLOTS):
        gains[i] = sent[0, i] + received[0, i]
    outside = received.at[0]
    for x in range(NX):
        for h in HALVES:
            total = plane(diag, h, x) + fine_z(outside, h, x) + fine_xy(outside, h, x)
            put(diag, h, x, total)
            put(inverse, h, x, 1.0 / total)
    for x in range(CX):
        for h in HALVES:
            put(coarse_inverse, h, x, 1.0 / (plane(coarse_diag, h, x) + coarse_z(outside, h, x) + coarse_xy(outside, h, x)))

    def residual_terms(turn, axis):
        for face in AXES[axis]:
            for i in range(OFFSETS[face], OFFSETS[face] + FINE[face]):
                term = gains[i] * received[turn, i]
                if turn == 1:
                    term = term - received[0, i] * sent[1, i]
                faces[i] = term

    def field_terms(turn, axis):
        for face in AXES[axis]:
            for i in range(OFFSETS[face], OFFSETS[face] + BOTH[face]):
                faces[i] = scaled_gains[i] * received[turn, i]

    for iteration in range(2):
        last = iteration == 1
        turn = 2 * iteration + 1
        wait(turn, (2,))
        residual_terms(turn, 2)
        for x in range(NX):
            for h in HALVES:
                put(partial, h, x, plane(partial, h, x) + fine_z(faces, h, x))
        wait(turn, (0, 1))
        residual_terms(turn, 0)
        residual_terms(turn, 1)

        def smooth(x):
            for h in HALVES:
                pair = []
                for fx in (2 * x, 2 * x + 1):
                    r = plane(partial, h, fx) + fine_xy(faces, h, fx)
                    put(first, h, fx, FIRST_RATE * plane(inverse, h, fx) * r)
                    pair.append(r)
                put(coarse_first, h, x, 4.0 * FIRST_RATE * plane(coarse_inverse, h, x) * restrict(*pair))

        turn += 1
        smooth(0)
        smooth(CX - 1)
        pack_x(sent.at[turn], first, coarse_first)
        send(turn, 0)
        for x in range(1, CX - 1):
            smooth(x)
        pack_y(sent.at[turn], first, coarse_first)
        send(turn, 1)
        pack_z(sent.at[turn], first, coarse_first)
        send(turn, 2)

        if not last:
            for pack in (pack_x, pack_y, pack_z):
                pack(scaled_gains, inverse, coarse_inverse)
            for i in range(SLOTS):
                scaled_gains[i] = FRESH * scaled_gains[i] * gains[i]
        for x in range(CX):
            total = coarse_neighbours(coarse_first, x)
            coarse = [KEEP * plane(coarse_first, h, x) + FRESH * plane(coarse_inverse, h, x) * total[h] for h in HALVES]
            for fx in (2 * x, 2 * x + 1):
                total = fine_neighbours(first, fx)
                for h in HALVES:
                    fine = KEEP * plane(first, h, fx) + FRESH * plane(inverse, h, fx) * total[h]
                    put(partial, h, fx, plane(field, h, fx) + fine + coarse[h])
        wait_sent(turn - 1)
        if not last:
            wait_sent(0)

        wait(turn, (2,))
        field_terms(turn, 2)
        for x in range(CX):
            for h in HALVES:
                coarse = coarse_z(faces, h, x)
                for fx in (2 * x, 2 * x + 1):
                    put(partial, h, fx, plane(partial, h, fx) + coarse + fine_z(faces, h, fx))
        wait(turn, (0, 1))
        field_terms(turn, 0)
        field_terms(turn, 1)

        def update(x):
            for h in HALVES:
                coarse = coarse_xy(faces, h, x)
                for fx in (2 * x, 2 * x + 1):
                    value = plane(partial, h, fx) + coarse + fine_xy(faces, h, fx)
                    if last:
                        out[NY * fx : NY * (fx + 1), 128 * h : 128 * (h + 1)] = value.reshape(16, 128)
                    else:
                        put(field, h, fx, value)

        update(0)
        update(CX - 1)
        if not last:
            pack_x(sent.at[turn + 1], field)
            send(turn + 1, 0)
        for x in range(1, CX - 1):
            update(x)
        if not last:
            pack_y(sent.at[turn + 1], field)
            send(turn + 1, 1)
            pack_z(sent.at[turn + 1], field)
            send(turn + 1, 2)
            residual_part()
            wait_sent(turn)
    wait_sent(TURNS - 1)


def block(source_term, conductivity, initial_field):
    def fine():
        return pltpu.VMEM((2, ROWS, 128), F32)

    def coarse():
        return pltpu.VMEM((2, CX * NY, 128), F32)

    hbm = pl.BlockSpec(memory_space=pltpu.HBM)
    result = pl.pallas_call(
        kernel,
        out_shape=pltpu.VMEM((ROWS, NZ), F32),
        in_specs=[hbm] * 3,
        out_specs=pl.BlockSpec(memory_space=pltpu.VMEM),
        scratch_shapes=[
            *(fine() for _ in range(11)),
            *(coarse() for _ in range(8)),
            *(pltpu.VMEM((SLOTS, 8, 128), F32) for _ in range(3)),
            *(pltpu.VMEM((TURNS, SLOTS, 8, 128), F32) for _ in range(2)),
            pltpu.SemaphoreType.DMA((3, 2)),
            *(pltpu.SemaphoreType.DMA((TURNS, 6)) for _ in range(2)),
        ],
        compiler_params=pltpu.CompilerParams(collective_id=0, has_side_effects=True),
    )(*(a.reshape(ROWS, NZ) for a in (source_term, conductivity, initial_field)))
    return result.reshape(NX, NY, NZ)


def solution(mesh):
    spec = P("gx", "gy", "grp")
    return jax.shard_map(block, mesh=mesh, in_specs=(spec,) * 3, out_specs=spec, check_vma=False)
```

time: 23.9 us -> 23.5 us (0.983)
  the two profiles are of different devices: /device:TPU:213 before, /device:TPU:211 now
where the time goes in v3:
time: 23.5 us; the launch traced here: 23.4 us
  Pallas kernels  22.7 us (97%)
  local copies, waits for them, and re-layouts  0.66 us (3%)
    pallas_call x1, Pallas kernels, block(): pl.pallas_call(kernel, out_shape=pltpu.VMEM((ROWS, NZ), F32), in_specs=[h...  22.7 us
    unnamed x1, local copies, waits for them, and re-layouts  0.66 us

profile of v3, /device:TPU:211, one launch (start us, length us, event | category | flops | bytes accessed | tf_op | source)
XLA Modules:
  0.0 23.4 jit_solution(1080144684344102058)
XLA Ops:
  0.0 22.7 %shard_map.37 = f32[128,256]{1,0:T(8,128)S(1)} custom-call(f32[128,256]{1,0:T(8,128)} %bitcast.5, f32[128,256]{1,0:T(8,128)} %bitcast.6, f32[128,256]{1,0:T(8,128)} %bitcast.7), custom_call_target="tpu_custom_call" | custom-call | tf_op jit(solution)/shard_map/pallas_call | solution.py:415
  22.7 0.7 %copy.5 = f32[8,16,256]{2,1,0:T(8,128)} copy(f32[8,16,256]{2,1,0:T(8,128)S(1)} %bitcast.4) | data formatting | bytes 262144

commit v4 on v3

--- a/solution.py
+++ b/solution.py
@@ -39,10 +39,8 @@
            faces, gains, scaled_gains, sent, received, in_sem, send_sem, recv_sem):
     sub, lane = iota((2, 8, 128), 1), iota((2, 8, 128), 2)
     sub2, lane2 = iota((8, 128), 0), iota((8, 128), 1)
-    even_sub, even_lane = sub % 2 == 0, lane % 2 == 0
     even_sub2, even_lane2 = sub2 % 2 == 0, lane2 % 2 == 0
     zero = jnp.zeros((1, 8, 128), F32)
-    tile = iota((2, 8, 128), 0)
 
     place = {name: lax.axis_index(name) for name in ("grp", "gx", "gy")}
     size = {name: lax.axis_size(name) for name in ("grp", "gx", "gy")}
@@ -55,6 +53,12 @@
 
     def put(ref, half, x, value):
         ref[half, NY * x : NY * (x + 1), :] = value.reshape(16, 128)
+
+    def part(ref, half, x, t):
+        return ref[half, NY * x + 8 * t : NY * x + 8 * t + 8, :]
+
+    def put_part(ref, half, x, t, value):
+        ref[half, NY * x + 8 * t : NY * x + 8 * t + 8, :] = value
 
     def y_lower(p, width=1):
         rolled = pltpu.roll(p, width, 1)
@@ -111,8 +115,8 @@
 
     def restrict(lower, upper):
         s = lower + upper
-        s = s + jnp.where(even_sub, pltpu.roll(s, 7, 1), pltpu.roll(s, 1, 1))
-        s = s + jnp.where(even_lane, pltpu.roll(s, 127, 2), pltpu.roll(s, 1, 2))
+        s = s + jnp.where(even_sub2, pltpu.roll(s, 7, 0), pltpu.roll(s, 1, 0))
+        s = s + jnp.where(even_lane2, pltpu.roll(s, 127, 1), pltpu.roll(s, 1, 1))
         return 0.125 * s
 
     def slot(face, index):
@@ -131,12 +135,16 @@
                 dest[slot(face, 4)] = jnp.where(
                     even_sub2, jnp.where(even_lane2, p[0][0], p[1][0]), jnp.where(even_lane2, p[0][1], p[1][1]))
 
+    def pack_face_y(dest, face, fine, coarse=None):
+        row = (NY - 1) * (face - 2)
+        for h in HALVES:
+            dest[slot(face, h)] = fine[h, pl.ds(row, NX, stride=NY), :]
+            if coarse is not None:
+                dest[slot(face, 2), CX * h : CX * (h + 1), :] = coarse[h, pl.ds(row, CX, stride=NY), :]
+
     def pack_y(dest, fine, coarse=None):
-        for face, row in ((2, 0), (3, NY - 1)):
-            for h in HALVES:
-                dest[slot(face, h)] = fine[h, pl.ds(row, NX, stride=NY), :]
-                if coarse is not None:
-                    dest[slot(face, 2), CX * h : CX * (h + 1), :] = coarse[h, pl.ds(row, CX, stride=NY), :]
+        for face in AXES[1]:
+            pack_face_y(dest, face, fine, coarse)
 
     def pack_z(dest, fine, coarse=None):
         for face, h, source_lane in ((4, 0, 0), (5, 1, 127)):
@@ -151,44 +159,45 @@
                         packed = jnp.where(lane2 == m, pltpu.roll(p[t], (m - source_lane) % 128, 1), packed)
             dest[slot(face, 0)] = packed
 
-    def two(a, b):
-        return jnp.concatenate([a[None], b[None]], axis=0)
-
-    def fine_z(q, half, x):
-        column = q[slot(4 + half, 0)]
-        return jnp.where(lane == 127 * half, two(*(
-            jnp.broadcast_to(column[:, 2 * x + t : 2 * x + t + 1], (8, 128)) for t in TILES)), 0.0)
-
-    def coarse_z(q, half, x):
-        column = q[slot(4 + half, 0)]
-        return jnp.where(lane // 2 == 63 * half, two(*(
-            jnp.broadcast_to(column[:, 16 + 2 * x + t : 17 + 2 * x + t], (8, 128)) for t in TILES)), 0.0)
-
-    def fine_xy(q, half, x):
-        added = jnp.where(sub == 7 * tile, two(*(
-            jnp.broadcast_to(q[slot(face, half), x : x + 1, :], (8, 128)) for face in (2, 3))), 0.0)
+    def fine_z(q, half, x, t):
+        lanes = 2 * x + t
+        column = q[slot(4 + half, 0)][:, lanes : lanes + 1]
+        return jnp.where(lane2 == 127 * half, jnp.broadcast_to(column, (8, 128)), 0.0)
+
+    def coarse_z(q, half, x, t):
+        lanes = 16 + 2 * x + t
+        column = q[slot(4 + half, 0)][:, lanes : lanes + 1]
+        return jnp.where(lane2 // 2 == 63 * half, jnp.broadcast_to(column, (8, 128)), 0.0)
+
+    def fine_y(q, half, x, t):
+        return jnp.where(sub2 == 7 * t, jnp.broadcast_to(q[slot(2 + t, half), x : x + 1, :], (8, 128)), 0.0)
+
+    def coarse_y(q, half, x, t):
+        row = CX * half + x
+        return jnp.where(sub2 // 2 == 3 * t, jnp.broadcast_to(q[slot(2 + t, 2), row : row + 1, :], (8, 128)), 0.0)
+
+    def fine_xz(q, half, x, t):
+        added = fine_z(q, half, x, t)
         if x == 0:
-            added = added + q[slot(0, 2 * half) : slot(0, 2 * half) + 2]
+            added = added + q[slot(0, 2 * half + t)]
         if x == NX - 1:
-            added = added + q[slot(1, 2 * half) : slot(1, 2 * half) + 2]
+            added = added + q[slot(1, 2 * half + t)]
         return added
 
-    def coarse_plane(q, half, face):
+    def coarse_plane(q, half, face, t):
         packed = q[slot(face, 4)]
         if half == 0:
             p = jnp.where(even_lane2, packed, pltpu.roll(packed, 1, 1))
         else:
             p = jnp.where(even_lane2, pltpu.roll(packed, 127, 1), packed)
-        return two(jnp.where(even_sub2, p, pltpu.roll(p, 1, 0)), jnp.where(even_sub2, pltpu.roll(p, 7, 0), p))
-
-    def coarse_xy(q, half, x):
-        row = CX * half + x
-        added = jnp.where(sub // 2 == 3 * tile, two(*(
-            jnp.broadcast_to(q[slot(face, 2), row : row + 1, :], (8, 128)) for face in (2, 3))), 0.0)
+        return jnp.where(even_sub2, p, pltpu.roll(p, 1, 0)) if t == 0 else jnp.where(even_sub2, pltpu.roll(p, 7, 0), p)
+
+    def coarse_xz(q, half, x, t):
+        added = coarse_z(q, half, x, t)
         if x == 0:
-            added = added + coarse_plane(q, half, 0)
+            added = added + coarse_plane(q, half, 0, t)
         if x == CX - 1:
-            added = added + coarse_plane(q, half, 1)
+            added = added + coarse_plane(q, half, 1, t)
         return added
 
     def peer(face):
@@ -215,18 +224,17 @@
             device_id_type=MESH,
         )
 
-    def send(turn, axis):
-        for face in reversed(AXES[axis]):
+    def send(turn, faces_):
+        for face in faces_:
             @pl.when(present[face])
             def _():
                 copy(turn, face).start()
 
-    def wait(turn, axes):
-        for axis in axes:
-            for face in AXES[axis]:
-                @pl.when(present[face])
-                def _():
-                    arrival(turn, face).wait_recv()
+    def wait(turn, faces_):
+        for face in faces_:
+            @pl.when(present[face])
+            def _():
+                arrival(turn, face).wait_recv()
 
     def wait_sent(turn):
         for face in range(6):
@@ -263,17 +271,17 @@
             put(half_cond, h, x, 0.5 * plane(half_cond, h, x))
     for x in range(CX):
         for h in HALVES:
-            put(coarse_half, h, x, restrict(plane(half_cond, h, 2 * x), plane(half_cond, h, 2 * x + 1)))
+            for t in TILES:
+                put_part(coarse_half, h, x, t, restrict(part(half_cond, h, 2 * x, t), part(half_cond, h, 2 * x + 1, t)))
     for pack in (pack_x, pack_y, pack_z):
         pack(sent.at[0], half_cond, coarse_half)
     pl.semaphore_wait(barrier, sum(p.astype(jnp.int32) for p in present))
-    for axis in range(3):
-        send(0, axis)
+    send(0, (3, 2, 1, 0, 5, 4))
     for load in loads[1]:
         load.wait()
-    for axis, pack in enumerate((pack_x, pack_y, pack_z)):
+    for axis, pack in ((1, pack_y), (0, pack_x), (2, pack_z)):
         pack(sent.at[1], field)
-        send(1, axis)
+        send(1, AXES[axis])
 
     for x in range(NX):
         coefficients(half_cond, ky_lo, ky_hi, kz_lo, kz_hi, diag, x, NX, 1)
@@ -290,64 +298,67 @@
 
     residual_part()
 
-    wait(0, (2, 0, 1))
+    wait(0, (4, 5, 0, 1, 2, 3))
     for i in range(SLOTS):
         gains[i] = sent[0, i] + received[0, i]
     outside = received.at[0]
     for x in range(NX):
         for h in HALVES:
-            total = plane(diag, h, x) + fine_z(outside, h, x) + fine_xy(outside, h, x)
-            put(diag, h, x, total)
-            put(inverse, h, x, 1.0 / total)
+            for t in TILES:
+                total = part(diag, h, x, t) + fine_xz(outside, h, x, t) + fine_y(outside, h, x, t)
+                put_part(diag, h, x, t, total)
+                put_part(inverse, h, x, t, 1.0 / total)
     for x in range(CX):
         for h in HALVES:
-            put(coarse_inverse, h, x, 1.0 / (plane(coarse_diag, h, x) + coarse_z(outside, h, x) + coarse_xy(outside, h, x)))
-
-    def residual_terms(turn, axis):
-        for face in AXES[axis]:
+            for t in TILES:
+                total = part(coarse_diag, h, x, t) + coarse_xz(outside, h, x, t) + coarse_y(outside, h, x, t)
+                put_part(coarse_inverse, h, x, t, 1.0 / total)
+
+    def residual_terms(turn, faces_):
+        for face in faces_:
             for i in range(OFFSETS[face], OFFSETS[face] + FINE[face]):
                 term = gains[i] * received[turn, i]
                 if turn == 1:
                     term = term - received[0, i] * sent[1, i]
                 faces[i] = term
 
-    def field_terms(turn, axis):
-        for face in AXES[axis]:
+    def field_terms(turn, faces_):
+        for face in faces_:
             for i in range(OFFSETS[face], OFFSETS[face] + BOTH[face]):
                 faces[i] = scaled_gains[i] * received[turn, i]
 
     for iteration in range(2):
         last = iteration == 1
         turn = 2 * iteration + 1
-        wait(turn, (2,))
-        residual_terms(turn, 2)
+        near = (4, 5, 0, 1)
+        wait(turn, near)
+        residual_terms(turn, near)
         for x in range(NX):
             for h in HALVES:
-                put(partial, h, x, plane(partial, h, x) + fine_z(faces, h, x))
-        wait(turn, (0, 1))
-        residual_terms(turn, 0)
-        residual_terms(turn, 1)
-
-        def smooth(x):
+                for t in TILES:
+                    put_part(partial, h, x, t, part(partial, h, x, t) + fine_xz(faces, h, x, t))
+
+        def smooth(x, t):
             for h in HALVES:
                 pair = []
                 for fx in (2 * x, 2 * x + 1):
-                    r = plane(partial, h, fx) + fine_xy(faces, h, fx)
-                    put(first, h, fx, FIRST_RATE * plane(inverse, h, fx) * r)
+                    r = part(partial, h, fx, t) + fine_y(faces, h, fx, t)
+                    put_part(first, h, fx, t, FIRST_RATE * part(inverse, h, fx, t) * r)
                     pair.append(r)
-                put(coarse_first, h, x, 4.0 * FIRST_RATE * plane(coarse_inverse, h, x) * restrict(*pair))
-
+                put_part(coarse_first, h, x, t, 4.0 * FIRST_RATE * part(coarse_inverse, h, x, t) * restrict(*pair))
+
+        for t in TILES:
+            wait(turn, (2 + t,))
+            residual_terms(turn, (2 + t,))
+            for x in range(CX):
+                smooth(x, t)
+            pack_face_y(sent.at[turn + 1], 2 + t, first, coarse_first)
+            send(turn + 1, (2 + t,))
         turn += 1
-        smooth(0)
-        smooth(CX - 1)
         pack_x(sent.at[turn], first, coarse_first)
-        send(turn, 0)
-        for x in range(1, CX - 1):
-            smooth(x)
-        pack_y(sent.at[turn], first, coarse_first)
-        send(turn, 1)
+        send(turn, AXES[0])
         pack_z(sent.at[turn], first, coarse_first)
-        send(turn, 2)
+        send(turn, AXES[2])
 
         if not last:
             for pack in (pack_x, pack_y, pack_z):
@@ -366,39 +377,36 @@
         if not last:
             wait_sent(0)
 
-        wait(turn, (2,))
-        field_terms(turn, 2)
+        wait(turn, near)
+        field_terms(turn, near)
         for x in range(CX):
             for h in HALVES:
-                coarse = coarse_z(faces, h, x)
-                for fx in (2 * x, 2 * x + 1):
-                    put(partial, h, fx, plane(partial, h, fx) + coarse + fine_z(faces, h, fx))
-        wait(turn, (0, 1))
-        field_terms(turn, 0)
-        field_terms(turn, 1)
-
-        def update(x):
-            for h in HALVES:
-                coarse = coarse_xy(faces, h, x)
-                for fx in (2 * x, 2 * x + 1):
-                    value = plane(partial, h, fx) + coarse + fine_xy(faces, h, fx)
-                    if last:
-                        out[NY * fx : NY * (fx + 1), 128 * h : 128 * (h + 1)] = value.reshape(16, 128)
-                    else:
-                        put(field, h, fx, value)
-
-        update(0)
-        update(CX - 1)
+                for t in TILES:
+                    coarse = coarse_xz(faces, h, x, t)
+                    for fx in (2 * x, 2 * x + 1):
+                        put_part(partial, h, fx, t, part(partial, h, fx, t) + coarse + fine_xz(faces, h, fx, t))
+
+        for t in TILES:
+            wait(turn, (2 + t,))
+            field_terms(turn, (2 + t,))
+            for x in range(CX):
+                for h in HALVES:
+                    coarse = coarse_y(faces, h, x, t)
+                    for fx in (2 * x, 2 * x + 1):
+                        value = part(partial, h, fx, t) + coarse + fine_y(faces, h, fx, t)
+                        if last:
+                            row = NY * fx + 8 * t
+                            out[row : row + 8, 128 * h : 128 * (h + 1)] = value
+                        else:
+                            put_part(field, h, fx, t, value)
+            if not last:
+                pack_face_y(sent.at[turn + 1], 2 + t, field)
+                send(turn + 1, (2 + t,))
         if not last:
             pack_x(sent.at[turn + 1], field)
-            send(turn + 1, 0)
-        for x in range(1, CX - 1):
-            update(x)
-        if not last:
-            pack_y(sent.at[turn + 1], field)
-            send(turn + 1, 1)
+            send(turn + 1, AXES[0])
             pack_z(sent.at[turn + 1], field)
-            send(turn + 1, 2)
+            send(turn + 1, AXES[2])
             residual_part()
             wait_sent(turn)
     wait_sent(TURNS - 1)

time: 23.5 us -> 23.2 us (0.987)
  the two profiles are of different devices: /device:TPU:211 before, /device:TPU:219 now
where the time goes in v4:
time: 23.2 us; the launch traced here: 23 us
  Pallas kernels  22.4 us (97%)
  local copies, waits for them, and re-layouts  0.66 us (3%)
    pallas_call x1, Pallas kernels, block(): pl.pallas_call(kernel, out_shape=pltpu.VMEM((ROWS, NZ), F32), in_specs=[h...  22.4 us
    unnamed x1, local copies, waits for them, and re-layouts  0.66 us

profile of v4, /device:TPU:219, one launch (start us, length us, event | category | flops | bytes accessed | tf_op | source)
XLA Modules:
  0.0 23.0 jit_solution(3417363053052651932)
XLA Ops:
  0.0 22.4 %shard_map.37 = f32[128,256]{1,0:T(8,128)S(1)} custom-call(f32[128,256]{1,0:T(8,128)} %bitcast.5, f32[128,256]{1,0:T(8,128)} %bitcast.6, f32[128,256]{1,0:T(8,128)} %bitcast.7), custom_call_target="tpu_custom_call" | custom-call | tf_op jit(solution)/shard_map/pallas_call | solution.py:423
  22.4 0.7 %copy.5 = f32[8,16,256]{2,1,0:T(8,128)} copy(f32[8,16,256]{2,1,0:T(8,128)S(1)} %bitcast.4) | data formatting | bytes 262144

commit v5 on v4

--- a/solution.py
+++ b/solution.py
@@ -23,11 +23,12 @@
 FACES = (("gx", -1), ("gx", 1), ("gy", -1), ("gy", 1), ("grp", -1), ("grp", 1))
 BOTH = (5, 5, 3, 3, 1, 1)
 FINE = (4, 4, 2, 2, 1, 1)
-TURN_SIZES = (BOTH, FINE, BOTH, FINE, BOTH)
+TURN_SIZES = (BOTH, FINE, BOTH, FINE, BOTH, BOTH)
 TURNS = len(TURN_SIZES)
 OFFSETS = (0, 5, 10, 13, 16, 17)
 SLOTS = 18
 AXES = ((0, 1), (2, 3), (4, 5))
+EDGES = [(a, b) for p, q in ((0, 1), (0, 2), (1, 2)) for a in AXES[p] for b in AXES[q]]
 
 
 def iota(shape, dim):
@@ -36,7 +37,8 @@
 
 def kernel(source_hbm, cond_hbm, field_hbm, out, source, half_cond, field, first, ky_lo, ky_hi, kz_lo, kz_hi,
            diag, inverse, partial, coarse_half, cky_lo, cky_hi, ckz_lo, ckz_hi, coarse_diag, coarse_inverse, coarse_first,
-           faces, gains, scaled_gains, sent, received, in_sem, send_sem, recv_sem):
+           faces, gains, scaled_gains, beside, edge_sent, edge_received, sent,
+           received, in_sem, send_sem, recv_sem, edge_send_sem, edge_recv_sem):
     sub, lane = iota((2, 8, 128), 1), iota((2, 8, 128), 2)
     sub2, lane2 = iota((8, 128), 0), iota((8, 128), 1)
     even_sub2, even_lane2 = sub2 % 2 == 0, lane2 % 2 == 0
@@ -236,6 +238,138 @@
             def _():
                 arrival(turn, face).wait_recv()
 
+    def edge_copy(k, landing):
+        return pltpu.make_async_remote_copy(
+            src_ref=edge_sent.at[k],
+            dst_ref=edge_received.at[landing],
+            send_sem=edge_send_sem.at[k],
+            recv_sem=edge_recv_sem.at[landing],
+            device_id={**peer(EDGES[k][0]), **peer(EDGES[k][1])},
+            device_id_type=MESH,
+        )
+
+    edge_present = [jnp.logical_and(present[a], present[b]) for a, b in EDGES]
+
+    def send_edges(ks):
+        for k in ks:
+            a, b = EDGES[k]
+
+            @pl.when(edge_present[k])
+            def _():
+                edge_copy(k, EDGES.index((a ^ 1, b ^ 1))).start()
+
+    def wait_edges(ks):
+        for k in ks:
+            @pl.when(edge_present[k])
+            def _():
+                edge_copy(k, k).wait_recv()
+
+    def wait_sent_edges():
+        for k in range(len(EDGES)):
+            @pl.when(edge_present[k])
+            def _():
+                edge_copy(k, k).wait_send()
+
+    def row(ref, *index):
+        return jnp.broadcast_to(ref[index[0], index[1] : index[1] + 1, :], (8, 128))
+
+    def column(value, lane_):
+        return jnp.broadcast_to(value[:, lane_ : lane_ + 1], (8, 128))
+
+    def pack_edges(ks, turn):
+        cond, update = sent.at[0], sent.at[turn]
+        for k in ks:
+            a, b = EDGES[k]
+            if a < 2 and b < 4:
+                for h in HALVES:
+                    for j, ref in ((0, cond), (2, update)):
+                        x, i = (NX - 1) * a, CX * h + (CX - 1) * a
+                        edge_sent[k, j + h : j + h + 1, :] = ref[slot(b, h), x : x + 1, :]
+                        edge_sent[k, j + h + 4 : j + h + 5, :] = ref[slot(b, 2), i : i + 1, :]
+            elif a < 2:
+                c, u = cond[slot(b, 0)], update[slot(b, 0)]
+                fine, coarse = 2 * (NX - 1) * a, 16 + 2 * (CX - 1) * a
+                packed = pltpu.roll(u, (6 - coarse) % 128, 1)
+                packed = jnp.where(lane2 < 6, pltpu.roll(c, (4 - coarse) % 128, 1), packed)
+                packed = jnp.where(lane2 < 4, pltpu.roll(u, (2 - fine) % 128, 1), packed)
+                edge_sent[k] = jnp.where(lane2 < 2, pltpu.roll(c, (-fine) % 128, 1) if fine else c, packed)
+            else:
+                h, t = b - 4, a - 2
+                packed = pltpu.roll(update[slot(a, 2)], (35 - 127 * h) % 128, 1)
+                packed = jnp.where(lane2 < 35, pltpu.roll(cond[slot(a, 2)], (34 - 127 * h) % 128, 1), packed)
+                packed = jnp.where(lane2 < 34, pltpu.roll(update[slot(a, h)], (33 - 127 * h) % 128, 1), packed)
+                packed = jnp.where(lane2 < 33, pltpu.roll(cond[slot(a, h)], (32 - 127 * h) % 128, 1), packed)
+                rows = jnp.where(sub2 == 0, row(cond, slot(b, 0), 7 * t), row(update, slot(b, 0), 7 * t))
+                edge_sent[k] = jnp.where(lane2 < 32, rows, packed)
+
+    def add_edges(face):
+        def add(index, mask, c, u):
+            i = slot(face, index)
+            beside[i] = beside[i] + jnp.where(mask, (received[0, i] + c) * u, 0.0)
+
+        for side in range(6):
+            if side // 2 == face // 2:
+                continue
+            k = EDGES.index((min(face, side), max(face, side)))
+            if face < 2 and side < 4:
+                t = side - 2
+                r = [row(edge_received, k, j) for j in range(8)]
+                for h in HALVES:
+                    add(2 * h + t, sub2 == 7 * t, r[h], r[2 + h])
+                add(4, sub2 == 7 * t, jnp.where(even_lane2, r[4], r[5]), jnp.where(even_lane2, r[6], r[7]))
+            elif face < 2:
+                h = side - 4
+                lines = edge_received[k]
+                r = [column(lines, j) for j in range(8)]
+                for t in TILES:
+                    add(2 * h + t, lane2 == 127 * h, r[t], r[2 + t])
+                add(4, lane2 == 127 * h, jnp.where(even_sub2, r[4], r[5]), jnp.where(even_sub2, r[6], r[7]))
+            elif face < 4 and side < 2:
+                for h in HALVES:
+                    add(h, sub2 == 7 * side, row(edge_received, k, h), row(edge_received, k, 2 + h))
+                    add(2, sub2 == CX * h + (CX - 1) * side, row(edge_received, k, 4 + h), row(edge_received, k, 6 + h))
+            elif face < 4:
+                h = side - 4
+                lines = edge_received[k]
+                other = pltpu.roll(lines, 4, 0)
+                add(h, lane2 == 127 * h, column(lines, 32), column(lines, 33))
+                add(2, jnp.logical_and(lane2 // 2 == 63 * h, sub2 // 4 == h), column(other, 34), column(other, 35))
+            elif side < 2:
+                lines = edge_received[k]
+                for t in TILES:
+                    add(0, lane2 == 14 * side + t, column(lines, t), column(lines, 2 + t))
+                    add(0, lane2 == 16 + 6 * side + t, column(lines, 4 + t), column(lines, 6 + t))
+            else:
+                t = side - 2
+                shift = 1 if t else 127
+                c, u = (pltpu.roll(row(edge_received, k, j), shift, 1) for j in (0, 1))
+                fine = jnp.logical_and(sub2 == 7 * t, lane2 < 16)
+                coarse = jnp.logical_and(sub2 // 2 == 3 * t, jnp.logical_and(lane2 >= 16, lane2 < 24))
+                add(0, jnp.logical_and(jnp.logical_or(fine, coarse), lane2 % 2 == t), c, u)
+
+    def neighbour_field(face):
+        base = OFFSETS[face]
+        for i in range(base, base + BOTH[face]):
+            beside[i] = FRESH * received[4, i] * beside[i]
+        if face < 2:
+            for h in HALVES:
+                for t in TILES:
+                    i = slot(face, 2 * h + t)
+                    beside[i] = received[3, i] + beside[i] + coarse_plane(beside, h, face, t)
+        elif face < 4:
+            for h in HALVES:
+                spread = row(beside, slot(face, 2), CX * h)
+                for x in range(1, CX):
+                    spread = jnp.where(sub2 // 2 == x, row(beside, slot(face, 2), CX * h + x), spread)
+                beside[slot(face, h)] = received[3, slot(face, h)] + beside[slot(face, h)] + spread
+        else:
+            i = slot(face, 0)
+            value = beside[i]
+            spread = jnp.zeros((8, 128), F32)
+            for x in range(NX):
+                spread = jnp.where(lane2 // 2 == x, pltpu.roll(value, (2 * x - 16 - 2 * (x // 2)) % 128, 1), spread)
+            beside[i] = received[3, i] + value + spread
+
     def wait_sent(turn):
         for face in range(6):
             @pl.when(present[face])
@@ -263,6 +397,11 @@
             for turn in range(TURNS):
                 count = TURN_SIZES[turn][face]
                 received[turn, OFFSETS[face] : OFFSETS[face] + count] = jnp.zeros((count, 8, 128), F32)
+
+    for k in range(len(EDGES)):
+        @pl.when(jnp.logical_not(edge_present[k]))
+        def _():
+            edge_received[k] = jnp.zeros((8, 128), F32)
 
     for load in loads[0]:
         load.wait()
@@ -314,57 +453,22 @@
                 total = part(coarse_diag, h, x, t) + coarse_xz(outside, h, x, t) + coarse_y(outside, h, x, t)
                 put_part(coarse_inverse, h, x, t, 1.0 / total)
 
-    def residual_terms(turn, faces_):
-        for face in faces_:
-            for i in range(OFFSETS[face], OFFSETS[face] + FINE[face]):
-                term = gains[i] * received[turn, i]
-                if turn == 1:
-                    term = term - received[0, i] * sent[1, i]
-                faces[i] = term
-
-    def field_terms(turn, faces_):
-        for face in faces_:
-            for i in range(OFFSETS[face], OFFSETS[face] + BOTH[face]):
-                faces[i] = scaled_gains[i] * received[turn, i]
-
-    for iteration in range(2):
-        last = iteration == 1
-        turn = 2 * iteration + 1
-        near = (4, 5, 0, 1)
-        wait(turn, near)
-        residual_terms(turn, near)
+    def add_near(ref):
         for x in range(NX):
             for h in HALVES:
                 for t in TILES:
-                    put_part(partial, h, x, t, part(partial, h, x, t) + fine_xz(faces, h, x, t))
-
-        def smooth(x, t):
-            for h in HALVES:
-                pair = []
-                for fx in (2 * x, 2 * x + 1):
-                    r = part(partial, h, fx, t) + fine_y(faces, h, fx, t)
-                    put_part(first, h, fx, t, FIRST_RATE * part(inverse, h, fx, t) * r)
-                    pair.append(r)
-                put_part(coarse_first, h, x, t, 4.0 * FIRST_RATE * part(coarse_inverse, h, x, t) * restrict(*pair))
-
-        for t in TILES:
-            wait(turn, (2 + t,))
-            residual_terms(turn, (2 + t,))
-            for x in range(CX):
-                smooth(x, t)
-            pack_face_y(sent.at[turn + 1], 2 + t, first, coarse_first)
-            send(turn + 1, (2 + t,))
-        turn += 1
-        pack_x(sent.at[turn], first, coarse_first)
-        send(turn, AXES[0])
-        pack_z(sent.at[turn], first, coarse_first)
-        send(turn, AXES[2])
-
-        if not last:
-            for pack in (pack_x, pack_y, pack_z):
-                pack(scaled_gains, inverse, coarse_inverse)
-            for i in range(SLOTS):
-                scaled_gains[i] = FRESH * scaled_gains[i] * gains[i]
+                    put_part(ref, h, x, t, part(ref, h, x, t) + fine_xz(faces, h, x, t))
+
+    def smooth(x, t):
+        for h in HALVES:
+            pair = []
+            for fx in (2 * x, 2 * x + 1):
+                r = part(partial, h, fx, t) + fine_y(faces, h, fx, t)
+                put_part(first, h, fx, t, FIRST_RATE * part(inverse, h, fx, t) * r)
+                pair.append(r)
+            put_part(coarse_first, h, x, t, 4.0 * FIRST_RATE * part(coarse_inverse, h, x, t) * restrict(*pair))
+
+    def own_update():
         for x in range(CX):
             total = coarse_neighbours(coarse_first, x)
             coarse = [KEEP * plane(coarse_first, h, x) + FRESH * plane(coarse_inverse, h, x) * total[h] for h in HALVES]
@@ -373,42 +477,102 @@
                 for h in HALVES:
                     fine = KEEP * plane(first, h, fx) + FRESH * plane(inverse, h, fx) * total[h]
                     put(partial, h, fx, plane(field, h, fx) + fine + coarse[h])
-        wait_sent(turn - 1)
-        if not last:
-            wait_sent(0)
-
+
+    def update_terms(turn, faces_):
+        for face in faces_:
+            for i in range(OFFSETS[face], OFFSETS[face] + BOTH[face]):
+                faces[i] = scaled_gains[i] * received[turn, i]
+
+    def finish(turn, last):
         wait(turn, near)
-        field_terms(turn, near)
+        update_terms(turn, near)
         for x in range(CX):
             for h in HALVES:
                 for t in TILES:
                     coarse = coarse_xz(faces, h, x, t)
                     for fx in (2 * x, 2 * x + 1):
                         put_part(partial, h, fx, t, part(partial, h, fx, t) + coarse + fine_xz(faces, h, fx, t))
-
         for t in TILES:
             wait(turn, (2 + t,))
-            field_terms(turn, (2 + t,))
+            update_terms(turn, (2 + t,))
             for x in range(CX):
                 for h in HALVES:
                     coarse = coarse_y(faces, h, x, t)
                     for fx in (2 * x, 2 * x + 1):
                         value = part(partial, h, fx, t) + coarse + fine_y(faces, h, fx, t)
                         if last:
-                            row = NY * fx + 8 * t
-                            out[row : row + 8, 128 * h : 128 * (h + 1)] = value
+                            at = NY * fx + 8 * t
+                            out[at : at + 8, 128 * h : 128 * (h + 1)] = value
                         else:
                             put_part(field, h, fx, t, value)
-            if not last:
-                pack_face_y(sent.at[turn + 1], 2 + t, field)
-                send(turn + 1, (2 + t,))
-        if not last:
-            pack_x(sent.at[turn + 1], field)
-            send(turn + 1, AXES[0])
-            pack_z(sent.at[turn + 1], field)
-            send(turn + 1, AXES[2])
-            residual_part()
-            wait_sent(turn)
+
+    near = (4, 5, 0, 1)
+    every = near + (2, 3)
+
+    def first_terms(faces_):
+        for face in faces_:
+            for i in range(OFFSETS[face], OFFSETS[face] + FINE[face]):
+                faces[i] = gains[i] * received[1, i] - received[0, i] * sent[1, i]
+
+    wait(1, near)
+    first_terms(near)
+    add_near(partial)
+    for t in TILES:
+        wait(1, (2 + t,))
+        first_terms((2 + t,))
+        for x in range(CX):
+            smooth(x, t)
+        pack_face_y(sent.at[2], 2 + t, first, coarse_first)
+        send(2, (2 + t,))
+    pack_edges(range(4), 2)
+    send_edges(range(4))
+    pack_z(sent.at[2], first, coarse_first)
+    pack_edges(range(4, 12), 2)
+    send_edges(range(4, 12))
+    pack_x(sent.at[2], first, coarse_first)
+    send(2, near)
+
+    own_update()
+    pack_y(sent.at[3], partial)
+    send(3, AXES[1])
+    pack_x(sent.at[3], partial)
+    send(3, AXES[0])
+    pack_z(sent.at[3], partial)
+    send(3, AXES[2])
+    for axis, pack in ((1, pack_y), (0, pack_x), (2, pack_z)):
+        pack(sent.at[4], inverse, coarse_inverse)
+        send(4, AXES[axis])
+    for i in range(SLOTS):
+        scaled_gains[i] = FRESH * sent[4, i] * gains[i]
+        beside[i] = gains[i] * sent[2, i]
+    wait_sent(0)
+    wait_sent(1)
+    finish(2, False)
+    residual_part()
+
+    wait(3, every)
+    wait(4, every)
+    wait_edges(range(12))
+    for face in every:
+        add_edges(face)
+        neighbour_field(face)
+        for i in range(OFFSETS[face], OFFSETS[face] + FINE[face]):
+            faces[i] = gains[i] * beside[i]
+    add_near(partial)
+    for t in TILES:
+        for x in range(CX):
+            smooth(x, t)
+        pack_face_y(sent.at[5], 2 + t, first, coarse_first)
+        send(5, (2 + t,))
+    pack_x(sent.at[5], first, coarse_first)
+    send(5, AXES[0])
+    pack_z(sent.at[5], first, coarse_first)
+    send(5, AXES[2])
+    own_update()
+    for turn in (2, 3, 4):
+        wait_sent(turn)
+    wait_sent_edges()
+    finish(5, True)
     wait_sent(TURNS - 1)
 
 
@@ -428,10 +592,12 @@
         scratch_shapes=[
             *(fine() for _ in range(11)),
             *(coarse() for _ in range(8)),
-            *(pltpu.VMEM((SLOTS, 8, 128), F32) for _ in range(3)),
+            *(pltpu.VMEM((SLOTS, 8, 128), F32) for _ in range(4)),
+            *(pltpu.VMEM((len(EDGES), 8, 128), F32) for _ in range(2)),
             *(pltpu.VMEM((TURNS, SLOTS, 8, 128), F32) for _ in range(2)),
             pltpu.SemaphoreType.DMA((3, 2)),
             *(pltpu.SemaphoreType.DMA((TURNS, 6)) for _ in range(2)),
+            *(pltpu.SemaphoreType.DMA((len(EDGES),)) for _ in range(2)),
         ],
         compiler_params=pltpu.CompilerParams(collective_id=0, has_side_effects=True),
     )(*(a.reshape(ROWS, NZ) for a in (source_term, conductivity, initial_field)))

time: 23.2 us -> 22.1 us (0.953)
  Pallas kernels: 22.4 us -> 21.3 us
    pallas_call x1, Pallas kernels: 22.4 us -> 21.3 us  [block(): pl.pallas_call(kernel, out_shape=pltpu.VMEM((ROWS, NZ), F32), in_specs=[h...]
where the time goes in v5:
time: 22.1 us; the launch traced here: 22 us
  Pallas kernels  21.3 us (96%)
  local copies, waits for them, and re-layouts  0.66 us (3%)
    pallas_call x1, Pallas kernels, block(): pl.pallas_call(kernel, out_shape=pltpu.VMEM((ROWS, NZ), F32), in_specs=[h...  21.3 us
    unnamed x1, local copies, waits for them, and re-layouts  0.66 us

profile of v5, /device:TPU:219, one launch (start us, length us, event | category | flops | bytes accessed | tf_op | source)
XLA Modules:
  0.0 22.0 jit_solution(16643148536899893622)
XLA Ops:
  0.0 21.3 %shard_map.37 = f32[128,256]{1,0:T(8,128)S(1)} custom-call(f32[128,256]{1,0:T(8,128)} %bitcast.5, f32[128,256]{1,0:T(8,128)} %bitcast.6, f32[128,256]{1,0:T(8,128)} %bitcast.7), custom_call_target="tpu_custom_call" | custom-call | tf_op jit(solution)/shard_map/pallas_call | solution.py:587
  21.3 0.7 %copy.5 = f32[8,16,256]{2,1,0:T(8,128)} copy(f32[8,16,256]{2,1,0:T(8,128)S(1)} %bitcast.4) | data formatting | bytes 262144

commit v6 on v5

--- a/solution.py
+++ b/solution.py
@@ -302,14 +302,12 @@
                 rows = jnp.where(sub2 == 0, row(cond, slot(b, 0), 7 * t), row(update, slot(b, 0), 7 * t))
                 edge_sent[k] = jnp.where(lane2 < 32, rows, packed)
 
-    def add_edges(face):
+    def add_edges(face, sides):
         def add(index, mask, c, u):
             i = slot(face, index)
             beside[i] = beside[i] + jnp.where(mask, (received[0, i] + c) * u, 0.0)
 
-        for side in range(6):
-            if side // 2 == face // 2:
-                continue
+        for side in sides:
             k = EDGES.index((min(face, side), max(face, side)))
             if face < 2 and side < 4:
                 t = side - 2
@@ -523,9 +521,9 @@
         for x in range(CX):
             smooth(x, t)
         pack_face_y(sent.at[2], 2 + t, first, coarse_first)
-        send(2, (2 + t,))
     pack_edges(range(4), 2)
     send_edges(range(4))
+    send(2, AXES[1])
     pack_z(sent.at[2], first, coarse_first)
     pack_edges(range(4, 12), 2)
     send_edges(range(4, 12))
@@ -550,15 +548,36 @@
     finish(2, False)
     residual_part()
 
+    wait_edges(range(4, 12))
+    for face in near:
+        add_edges(face, (2, 3) if face >= 4 else (4, 5))
+    for face in AXES[1]:
+        add_edges(face, (4, 5))
+    for face in AXES[2]:
+        add_edges(face, (0, 1))
     wait(3, every)
     wait(4, every)
-    wait_edges(range(12))
-    for face in every:
-        add_edges(face)
-        neighbour_field(face)
-        for i in range(OFFSETS[face], OFFSETS[face] + FINE[face]):
-            faces[i] = gains[i] * beside[i]
-    add_near(partial)
+    def second_terms(faces_):
+        for face in faces_:
+            neighbour_field(face)
+            for i in range(OFFSETS[face], OFFSETS[face] + FINE[face]):
+                faces[i] = gains[i] * beside[i]
+
+    second_terms(AXES[2])
+    for x in range(NX):
+        for h in HALVES:
+            for t in TILES:
+                put_part(partial, h, x, t, part(partial, h, x, t) + fine_z(faces, h, x, t))
+    wait_edges(range(4))
+    for face in AXES[1]:
+        add_edges(face, (0, 1))
+    for face in AXES[0]:
+        add_edges(face, (2, 3))
+    second_terms((2, 3, 0, 1))
+    for face, x in ((0, 0), (1, NX - 1)):
+        for h in HALVES:
+            for t in TILES:
+                put_part(partial, h, x, t, part(partial, h, x, t) + faces[slot(face, 2 * h + t)])
     for t in TILES:
         for x in range(CX):
             smooth(x, t)

time: 22.1 us -> 22.1 us (level)
  no operation moved by 1% of the time
where the time goes in v6:
time: 22.1 us; the launch traced here: 21.9 us
  Pallas kernels  21.3 us (96%)
  local copies, waits for them, and re-layouts  0.66 us (3%)
    pallas_call x1, Pallas kernels, block(): pl.pallas_call(kernel, out_shape=pltpu.VMEM((ROWS, NZ), F32), in_specs=[h...  21.3 us
    unnamed x1, local copies, waits for them, and re-layouts  0.66 us

profile of v6, /device:TPU:219, one launch (start us, length us, event | category | flops | bytes accessed | tf_op | source)
XLA Modules:
  0.0 21.9 jit_solution(14173216631938503488)
XLA Ops:
  0.0 21.3 %shard_map.37 = f32[128,256]{1,0:T(8,128)S(1)} custom-call(f32[128,256]{1,0:T(8,128)} %bitcast.5, f32[128,256]{1,0:T(8,128)} %bitcast.6, f32[128,256]{1,0:T(8,128)} %bitcast.7), custom_call_target="tpu_custom_call" | custom-call | tf_op jit(solution)/shard_map/pallas_call | solution.py:606
  21.3 0.7 %copy.5 = f32[8,16,256]{2,1,0:T(8,128)} copy(f32[8,16,256]{2,1,0:T(8,128)S(1)} %bitcast.4) | data formatting | bytes 262144

commit v7 on v6

--- a/solution.py
+++ b/solution.py
@@ -413,10 +413,12 @@
     for pack in (pack_x, pack_y, pack_z):
         pack(sent.at[0], half_cond, coarse_half)
     pl.semaphore_wait(barrier, sum(p.astype(jnp.int32) for p in present))
-    send(0, (3, 2, 1, 0, 5, 4))
+    send(0, AXES[1])
     for load in loads[1]:
         load.wait()
     for axis, pack in ((1, pack_y), (0, pack_x), (2, pack_z)):
+        if axis != 1:
+            send(0, AXES[axis])
         pack(sent.at[1], field)
         send(1, AXES[axis])
 
@@ -523,10 +525,10 @@
         pack_face_y(sent.at[2], 2 + t, first, coarse_first)
     pack_edges(range(4), 2)
     send_edges(range(4))
-    send(2, AXES[1])
     pack_z(sent.at[2], first, coarse_first)
     pack_edges(range(4, 12), 2)
-    send_edges(range(4, 12))
+    send_edges((8, 9, 10, 11, 4, 5, 6, 7))
+    send(2, AXES[1])
     pack_x(sent.at[2], first, coarse_first)
     send(2, near)
 

time: 22.1 us -> 22.1 us (level)
  no operation moved by 1% of the time
where the time goes in v7:
time: 22.1 us; the launch traced here: 21.9 us
  Pallas kernels  21.3 us (96%)
  local copies, waits for them, and re-layouts  0.66 us (3%)
    pallas_call x1, Pallas kernels, block(): pl.pallas_call(kernel, out_shape=pltpu.VMEM((ROWS, NZ), F32), in_specs=[h...  21.3 us
    unnamed x1, local copies, waits for them, and re-layouts  0.66 us

profile of v7, /device:TPU:219, one launch (start us, length us, event | category | flops | bytes accessed | tf_op | source)
XLA Modules:
  0.0 21.9 jit_solution(5694459467874469515)
XLA Ops:
  0.0 21.3 %shard_map.37 = f32[128,256]{1,0:T(8,128)S(1)} custom-call(f32[128,256]{1,0:T(8,128)} %bitcast.5, f32[128,256]{1,0:T(8,128)} %bitcast.6, f32[128,256]{1,0:T(8,128)} %bitcast.7), custom_call_target="tpu_custom_call" | custom-call | tf_op jit(solution)/shard_map/pallas_call | solution.py:608
  21.3 0.7 %copy.5 = f32[8,16,256]{2,1,0:T(8,128)} copy(f32[8,16,256]{2,1,0:T(8,128)S(1)} %bitcast.4) | data formatting | bytes 262144

commit v8 on v7

--- a/solution.py
+++ b/solution.py
@@ -514,6 +514,9 @@
             for i in range(OFFSETS[face], OFFSETS[face] + FINE[face]):
                 faces[i] = gains[i] * received[1, i] - received[0, i] * sent[1, i]
 
+    for axis, pack in ((1, pack_y), (0, pack_x)):
+        pack(sent.at[4], inverse, coarse_inverse)
+        send(4, AXES[axis])
     wait(1, near)
     first_terms(near)
     add_near(partial)
@@ -539,9 +542,8 @@
     send(3, AXES[0])
     pack_z(sent.at[3], partial)
     send(3, AXES[2])
-    for axis, pack in ((1, pack_y), (0, pack_x), (2, pack_z)):
-        pack(sent.at[4], inverse, coarse_inverse)
-        send(4, AXES[axis])
+    pack_z(sent.at[4], inverse, coarse_inverse)
+    send(4, AXES[2])
     for i in range(SLOTS):
         scaled_gains[i] = FRESH * sent[4, i] * gains[i]
         beside[i] = gains[i] * sent[2, i]

time: 22.1 us -> 21.9 us (level)
  no operation moved by 1% of the time
where the time goes in v8:
time: 21.9 us; the launch traced here: 21.7 us
  Pallas kernels  21.1 us (96%)
  local copies, waits for them, and re-layouts  0.66 us (3%)
    pallas_call x1, Pallas kernels, block(): pl.pallas_call(kernel, out_shape=pltpu.VMEM((ROWS, NZ), F32), in_specs=[h...  21.1 us
    unnamed x1, local copies, waits for them, and re-layouts  0.66 us

profile of v8, /device:TPU:219, one launch (start us, length us, event | category | flops | bytes accessed | tf_op | source)
XLA Modules:
  0.0 21.7 jit_solution(15747548859266185056)
XLA Ops:
  0.0 21.1 %shard_map.37 = f32[128,256]{1,0:T(8,128)S(1)} custom-call(f32[128,256]{1,0:T(8,128)} %bitcast.5, f32[128,256]{1,0:T(8,128)} %bitcast.6, f32[128,256]{1,0:T(8,128)} %bitcast.7), custom_call_target="tpu_custom_call" | custom-call | tf_op jit(solution)/shard_map/pallas_call | solution.py:610
  21.1 0.7 %copy.5 = f32[8,16,256]{2,1,0:T(8,128)} copy(f32[8,16,256]{2,1,0:T(8,128)S(1)} %bitcast.4) | data formatting | bytes 262144

commit v9 on v8

--- a/solution.py
+++ b/solution.py
@@ -375,7 +375,7 @@
                 copy(turn, face).wait_send()
 
     barrier = pltpu.get_barrier_semaphore()
-    for face in range(6):
+    for face in (3, 2, 1, 0, 5, 4):
         @pl.when(present[face])
         def _():
             pl.semaphore_signal(barrier, inc=1, device_id=peer(face), device_id_type=MESH)
@@ -410,13 +410,15 @@
         for h in HALVES:
             for t in TILES:
                 put_part(coarse_half, h, x, t, restrict(part(half_cond, h, 2 * x, t), part(half_cond, h, 2 * x + 1, t)))
-    for pack in (pack_x, pack_y, pack_z):
+    for pack in (pack_y, pack_x):
         pack(sent.at[0], half_cond, coarse_half)
     pl.semaphore_wait(barrier, sum(p.astype(jnp.int32) for p in present))
     send(0, AXES[1])
     for load in loads[1]:
         load.wait()
     for axis, pack in ((1, pack_y), (0, pack_x), (2, pack_z)):
+        if axis == 2:
+            pack(sent.at[0], half_cond, coarse_half)
         if axis != 1:
             send(0, AXES[axis])
         pack(sent.at[1], field)

time: 21.9 us -> 21.9 us (level)
  no operation moved by 1% of the time
where the time goes in v9:
time: 21.9 us; the launch traced here: 21.7 us
  Pallas kernels  21.1 us (96%)
  local copies, waits for them, and re-layouts  0.66 us (3%)
    pallas_call x1, Pallas kernels, block(): pl.pallas_call(kernel, out_shape=pltpu.VMEM((ROWS, NZ), F32), in_specs=[h...  21.1 us
    unnamed x1, local copies, waits for them, and re-layouts  0.66 us

profile of v9, /device:TPU:219, one launch (start us, length us, event | category | flops | bytes accessed | tf_op | source)
XLA Modules:
  0.0 21.7 jit_solution(11550255906125368866)
XLA Ops:
  0.0 21.1 %shard_map.37 = f32[128,256]{1,0:T(8,128)S(1)} custom-call(f32[128,256]{1,0:T(8,128)} %bitcast.5, f32[128,256]{1,0:T(8,128)} %bitcast.6, f32[128,256]{1,0:T(8,128)} %bitcast.7), custom_call_target="tpu_custom_call" | custom-call | tf_op jit(solution)/shard_map/pallas_call | solution.py:612
  21.1 0.7 %copy.5 = f32[8,16,256]{2,1,0:T(8,128)} copy(f32[8,16,256]{2,1,0:T(8,128)S(1)} %bitcast.4) | data formatting | bytes 262144

commit v10 on v9

--- a/solution.py
+++ b/solution.py
@@ -597,8 +597,8 @@
     for turn in (2, 3, 4):
         wait_sent(turn)
     wait_sent_edges()
+    wait_sent(TURNS - 1)
     finish(5, True)
-    wait_sent(TURNS - 1)
 
 
 def block(source_term, conductivity, initial_field):

time: 21.9 us -> 21.9 us (level)
  no operation moved by 1% of the time
where the time goes in v10:
time: 21.9 us; the launch traced here: 21.7 us
  Pallas kernels  21.1 us (96%)
  local copies, waits for them, and re-layouts  0.66 us (3%)
    pallas_call x1, Pallas kernels, block(): pl.pallas_call(kernel, out_shape=pltpu.VMEM((ROWS, NZ), F32), in_specs=[h...  21.1 us
    unnamed x1, local copies, waits for them, and re-layouts  0.66 us

profile of v10, /device:TPU:219, one launch (start us, length us, event | category | flops | bytes accessed | tf_op | source)
XLA Modules:
  0.0 21.7 jit_solution(6666403301501507449)
XLA Ops:
  0.0 21.1 %shard_map.37 = f32[128,256]{1,0:T(8,128)S(1)} custom-call(f32[128,256]{1,0:T(8,128)} %bitcast.5, f32[128,256]{1,0:T(8,128)} %bitcast.6, f32[128,256]{1,0:T(8,128)} %bitcast.7), custom_call_target="tpu_custom_call" | custom-call | tf_op jit(solution)/shard_map/pallas_call | solution.py:612
  21.1 0.7 %copy.5 = f32[8,16,256]{2,1,0:T(8,128)} copy(f32[8,16,256]{2,1,0:T(8,128)S(1)} %bitcast.4) | data formatting | bytes 262144
